TPU v7x, 256 devices: a whole 4x4x8 slice. The times are simulated.
256 devices in a mesh: space: 128 (over y, z, x), tm: 2 (over core).
Axes of the slice: x: 4, y: 4, z: 8, core: 2. Of those that a mesh axis runs over, the one named last changes fastest.
Arguments:
- snapshots: bfloat16 [2097152, 512], P(('space', 'tm')), may hold values from -6 to 6
- range_test: bfloat16 [512, 128], replicated, may hold values from -0.25 to 0.25
- test_rows: bfloat16 [256, 2097152], P(None, ('space', 'tm')), may hold values from -0.00390625 to 0.00390625
- species: int32 [2048, 1024], P(('space', 'tm')), may hold values from 0 to 3
- reaction_rates: float32 [4], replicated, may hold values from 1 to 8
- adjoint_end: float32 [2048, 1024], P(('space', 'tm')), may hold values from -6 to 6
Outputs:
- adjoint: float32 [2048, 1024], P(('space', 'tm'))
- time_factors: float32 [128, 512], P(None, ('space', 'tm'))
All inputs are finite; a program needn't handle non-finite values.
Results may differ from a plain program's by a relative error of at most 0.0012.
Values sent between devices are 32-bit elements; how exact they have to be, the bound alone decides.
A program may use at most 64 MiB of HBM per device.

v0:
```python
import jax
import jax.numpy as jnp
from jax import lax
from jax.sharding import Mesh
from jax.sharding import PartitionSpec as P

SPACE_TM = ("space_0", "space_1", "space_2", "tm")


DIFFUSION = 0.2
STEP_SIZE = 0.05


def with_halo(block, sides, width):
    for axis, dim in sides:
        count = lax.axis_size(axis)
        forward = [(i, i + 1) for i in range(count - 1)]
        backward = [(target, source) for source, target in forward]
        low = lax.ppermute(
            lax.slice_in_dim(block, block.shape[dim] - width, None, axis=dim), axis, forward
        )
        high = lax.ppermute(lax.slice_in_dim(block, 0, width, axis=dim), axis, backward)
        block = jnp.concatenate([low, block, high], axis=dim)
    return block


def together(arrays, axis):
    vector, at, done = (jnp.concatenate([a.reshape(-1) for a in arrays]), 0, [])
    running = lax.psum(vector, axis)
    for a in arrays:
        done.append(running[at : at + a.size].reshape(a.shape))
        at += a.size
    return tuple(done)


def from_root(value, axes, root):
    value = jnp.where(lax.axis_index(axes) == root, value, jnp.zeros_like(value))
    for axis in axes:
        value = lax.psum(value, axis)
    return value


def reverse_step(adjoint, state, coupling):
    padded = with_halo(adjoint, ((SPACE_TM, 0),), 1)
    sideways = jnp.pad(adjoint, ((0, 0), (1, 1)))
    laplace = padded[2:] + padded[:-2] + sideways[:, 2:] + sideways[:, :-2] - 4.0 * adjoint
    return (
        adjoint + DIFFUSION * laplace + STEP_SIZE * coupling * (1.0 - 3.0 * state * state) * adjoint
    )


def shards(snapshots, range_test, test_rows, species, reaction_rates, adjoint_end):
    high = lax.Precision.HIGHEST
    contract_rows = (((0,), (0,)), ((), ()))
    range_part = jnp.dot(snapshots, range_test, preferred_element_type=jnp.float32)
    gram_local = lax.dot_general(range_part, range_part, contract_rows, precision=high)
    raw_local = jnp.dot(test_rows, range_part, precision=high, preferred_element_type=jnp.float32)
    gram, projected_raw = together((gram_local, raw_local), SPACE_TM)
    lower_factor = jnp.linalg.cholesky(gram)
    basis = jax.scipy.linalg.solve_triangular(lower_factor, range_part.T, lower=True).T
    projected = jax.scipy.linalg.solve_triangular(lower_factor, projected_raw.T, lower=True).T
    devices = lax.axis_size(SPACE_TM)
    normal_matrix = lax.dot_general(projected, projected, contract_rows, precision=high)
    normal_factor = jnp.linalg.cholesky(normal_matrix)
    corange_local = jnp.dot(test_rows, snapshots, preferred_element_type=jnp.float32)
    corange_mine = lax.psum_scatter(corange_local, SPACE_TM, scatter_dimension=1, tiled=True)
    right_side = lax.dot_general(projected, corange_mine, contract_rows, precision=high)
    factors_mine = jax.scipy.linalg.cho_solve((normal_factor, True), right_side)
    cells_total = snapshots.shape[0] * devices
    time_factors = factors_mine * cells_total ** (-0.5)
    owner_part = from_root(factors_mine, SPACE_TM, devices - 1)
    states = jnp.dot(basis, owner_part, precision=high)
    rows_here = adjoint_end.shape[0]
    width_here = adjoint_end.shape[1]
    kinds = jnp.arange(reaction_rates.shape[0], dtype=jnp.int32)
    coupling = jnp.sum(jnp.where(species[:, :, None] == kinds, reaction_rates, 0.0), axis=-1)
    adjoint = adjoint_end
    for column in (1, 0):
        state = states[:, column].reshape(rows_here, width_here)
        adjoint = reverse_step(adjoint, state, coupling)
    return (adjoint, time_factors)


def solution(mesh):
    finer = Mesh(
        mesh.devices.reshape(4, 8, 4, mesh.shape["tm"]), ("space_0", "space_1", "space_2", "tm")
    )
    in_specs = (
        P(SPACE_TM, None),
        P(),
        P(None, SPACE_TM),
        P(SPACE_TM, None),
        P(),
        P(SPACE_TM, None),
    )
    out_specs = (P(SPACE_TM, None), P(None, SPACE_TM))
    return jax.shard_map(
        shards, mesh=finer, in_specs=in_specs, out_specs=out_specs, check_vma=False
    )
```

profile of v0, /device:TPU:1, one launch (start us, length us, event | category | flops | bytes accessed | tf_op | source)
XLA Modules:
  0.0 404.8 jit_solution(13783514176639291139)
XLA Ops:
  7.2 0.8 copy-done
  8.1 5.7 %fusion.37 = f32[8192,128]{1,0:T(8,128)S(1)} fusion(bf16[8192,512]{1,0:T(8,128)(2,1)} %param.7, bf16[512,128]{1,0:T(8,128)(2,1)S(1)} %copy-done), kind=kOutput, calls=%fused_computation.68 | convolution fusion | flops 1073741824 | bytes 12713984 | tf_op jit(solution)/shard_map/dot_general | solution.py:55
  13.8 6.9 %convolution_bitcast_fusion = f32[16384]{0:T(1024)S(1)} fusion(f32[8192,128]{1,0:T(8,128)S(1)} %fusion.37), kind=kOutput, calls=%fused_computation | convolution fusion | flops 1610612736 | bytes 4259840 | tf_op jit(solution)/shard_map/dot_general | solution.py:56
  20.8 3.6 convolution_bitcast_fusion.1
  24.4 3.1 fusion.39
  28.4 5.1 %collective-permute-start = (f32[1,1024]{1,0:T(1,128)S(1)}, f32[1,1024]{1,0:T(1,128)S(1)}, u32[]{:S(2)}, u32[]{:S(2)}) collective-permute-start(f32[1,1024]{1,0:T(1,128)S(1)} %get-tuple-element.9), channel_id=1, source_target_pairs={{1,0},{2,1},{3,2},{4,3},{5,4},{6,5},{7,6},{8,7},{9,8},{10,9},{11,1... | collective-permute-start | bytes 12296 | tf_op jit(solution)/shard_map/ppermute | solution.py:22
  33.5 1.9 collective-permute-start.1
  35.6 251.9 %all-reduce.6.cloned.1.call-done = (f32[49152]{0:T(1024)}, f32[256,512]{1,0:T(8,128)}) async-done(((f32[49152]{0:T(1024)}, f32[256,512]{1,0:T(8,128)}), (f32[49152]{0:T(1024)}, f32[256,512]{1,0:T(8,128)})) %all-reduce.6.cloned.1.call-update) | async-done | bytes 720912 | tf_op jit(solution)/shard_map/psum | solution.py:29
  287.5 0.8 slice_bitcast_fusion.2
  288.4 0.9 fusion.13
  289.3 11.7 %cholesky.44 = f32[128,128]{1,0:T(8,128)S(1)} custom-call(f32[128,128]{1,0:T(8,128)S(1)} %fusion.13), custom_call_target="Cholesky" | custom-call | tf_op jit(solution)/shard_map/jit(cholesky)/cholesky | solution.py:59
  302.4 9.8 %custom-call.16 = f32[1,128,128]{1,2,0:T(8,128)S(1)} custom-call(f32[1,128,128]{2,1,0:T(8,128)S(1)} %fusion.3), custom_call_target="InvertDiagBlocksLowerTriangular" | custom-call | tf_op jit(solution)/shard_map/jit(_solve_triangular)/triangular_solve | solution.py:60
  312.2 1.2 fusion
  313.4 7.9 %fusion.11 = f32[128,8192]{1,0:T(8,128)} fusion(f32[8192,128]{1,0:T(8,128)} %copy-done.1, f32[1,128,128]{1,2,0:T(8,128)S(1)} %custom-call.16), kind=kOutput, calls=%fused_computation.21 | convolution fusion | flops 1610612736 | bytes 8454144 | tf_op jit(solution)/shard_map/jit(_solve_triangular)/triangular_solve | solution.py:60
  321.7 11.9 %cholesky.55 = f32[128,128]{1,0:T(8,128)S(1)} custom-call(f32[128,128]{1,0:T(8,128)S(1)} %fusion.9), custom_call_target="Cholesky" | custom-call | tf_op jit(solution)/shard_map/jit(cholesky)/cholesky | solution.py:64
  335.0 9.8 %custom-call.17 = f32[1,128,128]{1,2,0:T(8,128)S(1)} custom-call(f32[1,128,128]{2,1,0:T(8,128)S(1)} %fusion.4), custom_call_target="InvertDiagBlocksLowerTriangular" | custom-call | tf_op jit(solution)/shard_map/jit(_cho_solve)/triangular_solve | solution.py:68
  344.8 1.3 fusion.1
  347.1 8.2 %psum.36 = f32[128,2]{0,1:T(2,128)S(1)} all-reduce(f32[128,2]{0,1:T(2,128)S(1)} %get-tuple-element.12), channel_id=1, replica_groups=mesh['space_0'=4,'space_1'=8,'space_2'=4,'tm'=2] {'space_0'}, use_global_device_ids=true, to_apply=%region_5.7 | all-reduce | flops 256 | bytes 2048 | tf_op jit(solution)/shard_map/psum | solution.py:39
  355.3 15.2 %psum.37 = f32[128,2]{0,1:T(2,128)S(1)} all-reduce(f32[128,2]{0,1:T(2,128)S(1)} %psum.36), channel_id=1, replica_groups=mesh['space_0'=4,'space_1'=8,'space_2'=4,'tm'=2] {'space_1'}, use_global_device_ids=true, to_apply=%region_6.8 | all-reduce | flops 256 | bytes 2048 | tf_op jit(solution)/shard_map/psum | solution.py:39
  370.5 6.3 %psum.38 = f32[128,2]{0,1:T(2,128)S(1)} all-reduce(f32[128,2]{0,1:T(2,128)S(1)} %psum.37), channel_id=1, replica_groups=mesh['space_0'=4,'space_1'=8,'space_2'=4,'tm'=2] {'space_2'}, use_global_device_ids=true, to_apply=%region_7.9 | all-reduce | flops 256 | bytes 2048 | tf_op jit(solution)/shard_map/psum | solution.py:39
  376.8 9.4 %psum.39 = f32[128,2]{0,1:T(2,128)S(1)} all-reduce(f32[128,2]{0,1:T(2,128)S(1)} %psum.38), channel_id=1, replica_groups=mesh['space_0'=4,'space_1'=8,'space_2'=4,'tm'=2] {'tm'}, use_global_device_ids=true, to_apply=%region_8.10 | all-reduce | flops 256 | bytes 2048 | tf_op jit(solution)/shard_map/psum | solution.py:39
  386.2 4.4 %fusion.40 = f32[8192,2]{0,1:T(2,128)S(1)} fusion(f32[128,8192]{1,0:T(8,128)} %fusion.11, f32[128,2]{0,1:T(2,128)S(1)} %psum.39), kind=kOutput, calls=%fused_computation.71 | convolution fusion | flops 25165824 | bytes 4260864 | tf_op jit(solution)/shard_map/dot_general | solution.py:72
  390.9 2.3 collective-permute-start.2
  393.2 3.3 collective-permute-start.3
  (44 shorter events, 6.8 us)
Async XLA Ops:
  7.2 0.9 copy-start
  7.2 280.3 %all-reduce.6.cloned.1.call-start = ((), (), s32[]{:S(2)}) async-start(), calls=%async_computation | async-start | bytes 1441792 | tf_op jit(solution)/shard_map/psum | solution.py:29
  13.8 6.9 %copy-start.1 = (f32[8192,128]{1,0:T(8,128)}, f32[8192,128]{1,0:T(8,128)S(1)}, u32[]{:S(2)}) copy-start(f32[8192,128]{1,0:T(8,128)S(1)} %fusion.37) | copy-start | bytes 12582916
  13.8 6.9 %copy-start.2 = (bf16[256,8192]{1,0:T(8,128)(2,1)S(1)}, bf16[256,8192]{1,0:T(8,128)(2,1)}, u32[]{:S(2)}) copy-start(bf16[256,8192]{1,0:T(8,128)(2,1)} %param.9) | copy-start | bytes 12582916
  13.8 10.6 %slice-start = ((s8[8388608]{0:T(1024)(128)(4,1)}), s8[4194304]{0:T(1024)(128)(4,1)S(1)}, s32[]{:S(2)}) async-start(s8[8388608]{0:T(1024)(128)(4,1)} %bitcast.54), calls=%async_computation.1 | async-start | bytes 8388608
  20.8 3.6 slice-start.1
  24.4 4.0 copy-start.3
  24.4 11.1 %copy-start.4 = (s32[8,1024]{1,0:T(8,128)S(1)}, s32[8,1024]{1,0:T(8,128)}, u32[]{:S(2)}) copy-start(s32[8,1024]{1,0:T(8,128)} %param.10) | copy-start | bytes 98308
  24.4 11.1 %copy-start.5 = (f32[4]{0:T(128)S(1)}, f32[4]{0:T(128)}, u32[]{:S(2)}) copy-start(f32[4]{0:T(128)} %param.11) | copy-start | bytes 52
  28.4 362.4 %collective-permute-start = (f32[1,1024]{1,0:T(1,128)S(1)}, f32[1,1024]{1,0:T(1,128)S(1)}, u32[]{:S(2)}, u32[]{:S(2)}) collective-permute-start(f32[1,1024]{1,0:T(1,128)S(1)} %get-tuple-element.9), channel_id=1, source_target_pairs={{1,0},{2,1},{3,2},{4,3},{5,4},{6,5},{7,6},{8,7},{9,8},{10,9},{11,1... | collective-permute-start | bytes 12296 | tf_op jit(solution)/shard_map/ppermute | solution.py:22
  33.5 357.3 %collective-permute-start.1 = (f32[1,1024]{1,0:T(1,128)S(1)}, f32[1,1024]{1,0:T(1,128)S(1)}, u32[]{:S(2)}, u32[]{:S(2)}) collective-permute-start(f32[1,1024]{1,0:T(1,128)S(1)} %get-tuple-element.10), channel_id=1, source_target_pairs={{0,1},{1,2},{2,3},{3,4},{4,5},{5,6},{6,7},{7,8},{8,9},{9,10},{10,1... | collective-permute-start | bytes 12296 | tf_op jit(solution)/shard_map/ppermute | solution.py:19
  390.9 5.6 %collective-permute-start.2 = (f32[1,1024]{1,0:T(1,128)S(1)}, f32[1,1024]{1,0:T(1,128)S(1)}, u32[]{:S(2)}, u32[]{:S(2)}) collective-permute-start(f32[1,1024]{1,0:T(1,128)S(1)} %get-tuple-element.7), channel_id=1, source_target_pairs={{1,0},{2,1},{3,2},{4,3},{5,4},{6,5},{7,6},{8,7},{9,8},{10,9},{11,1... | collective-permute-start | bytes 12296 | tf_op jit(solution)/shard_map/ppermute | solution.py:22
  393.2 4.1 %collective-permute-start.3 = (f32[1,1024]{1,0:T(1,128)S(1)}, f32[1,1024]{1,0:T(1,128)S(1)}, u32[]{:S(2)}, u32[]{:S(2)}) collective-permute-start(f32[1,1024]{1,0:T(1,128)S(1)} %get-tuple-element.8), channel_id=1, source_target_pairs={{0,1},{1,2},{2,3},{3,4},{4,5},{5,6},{6,7},{7,8},{8,9},{9,10},{10,1... | collective-permute-start | bytes 12296 | tf_op jit(solution)/shard_map/ppermute | solution.py:19
Sparse Core Ops, SparseCore 0:
  28.5 258.9 all-reduce.5
where the time goes:
time: 410 us; the launch traced here: 405 us
  waiting for transfers between devices  253 us (62%)
  other arithmetic  48.4 us (12%)
  blocking collectives  39.1 us (10%)
  matrix products  35.5 us (9%)
  between operations  14.4 us (4%)
  starting transfers between devices  12.6 us (3%)
    psum x1, waiting for transfers between devices, together(): running = lax.psum(vector, axis)  252 us
    psum x4, blocking collectives, from_root(): value = lax.psum(value, axis)  39.1 us
    another operation x3, other arithmetic, shards(): normal_factor = jnp.linalg.cholesky(normal_matrix)  12.6 us
    another operation x3, other arithmetic, shards(): lower_factor = jnp.linalg.cholesky(gram)  12.4 us
    another operation x2, other arithmetic, shards(): jax.scipy.linalg.solve_triangular(lower_factor, range_part.T, lower=True)  10.5 us
    another operation x2, other arithmetic, shards(): factors_mine = jax.scipy.linalg.cho_solve((normal_factor, True), right_side)  10.5 us
  transfers between devices with their start and end apart: 5, of which 2 were waited for; matrix products, arithmetic and copies ran while one was open for 16% of the time, Pallas kernels for 0%

commit v1 on v0

v1 whole, which is shorter than its diff:
```python
import functools

import jax
import jax.numpy as jnp
from jax import lax
from jax.experimental import pallas as pl
from jax.experimental.pallas import tpu as pltpu
from jax.sharding import PartitionSpec as P

DIFFUSION = 0.2
STEP_SIZE = 0.05
MESH = pl.DeviceIdType.MESH
HIGH = lax.Precision.HIGHEST
F32 = jnp.float32
BF16 = jnp.bfloat16

YS, ZS, XS, CS = 4, 8, 4, 2
PLANE = YS * XS * CS
STEPS = 8


def iota(shape, dim):
    return lax.broadcasted_iota(jnp.int32, shape, dim)


def local_kernel(x_ref, psi_ref, om_ref, ar_ref, ct_ref, yt_ref, c_acc, k_acc):
    step = pl.program_id(0)
    x = x_ref[...]
    corange = jnp.dot(psi_ref[...], x, preferred_element_type=F32)
    y = jnp.dot(x, om_ref[...], preferred_element_type=F32)
    yt = y.T
    yt_ref[...] = yt
    hi = y.astype(BF16)
    lo = (y - hi.astype(F32)).astype(BF16)
    hi_t = yt.astype(BF16)
    lo_t = (yt - hi_t.astype(F32)).astype(BF16)
    wide = jnp.concatenate([hi, lo], axis=1)
    wide_t = jnp.concatenate([hi_t, lo_t], axis=0)
    squares = jnp.dot(wide_t, wide, preferred_element_type=F32)

    @pl.when(step == 0)
    def _():
        c_acc[...] = corange
        k_acc[...] = squares

    @pl.when(step > 0)
    def _():
        c_acc[...] += corange
        k_acc[...] += squares

    @pl.when(step == pl.num_programs(0) - 1)
    def _():
        r = RANK = 128
        gram = (
            k_acc[0:r, 0:r] + k_acc[0:r, r : 2 * r] + k_acc[r : 2 * r, 0:r]
            + k_acc[r : 2 * r, r : 2 * r]
        )
        raw = jnp.dot(c_acc[...], om_ref[...].astype(F32), precision=HIGH)
        ar_ref[:, 0:8, :] = raw.reshape(PLANE, 8, RANK)
        row = iota((128, 128), 0)
        source = ((row >> 1) & 7) * 16 + ((row >> 5) & 3) * 4 + ((row >> 4) & 1) * 2 + (row & 1)
        perm = jnp.where(iota((128, 128), 1) == source, 1.0, 0.0).astype(F32)
        for y_at in range(YS):
            block = lax.dot_general(
                perm,
                c_acc[:, y_at * 128 : (y_at + 1) * 128],
                (((1,), (1,)), ((), ())),
                precision=HIGH,
                preferred_element_type=F32,
            )
            ct_ref[8 * y_at : 8 * y_at + 8] = block.reshape(8, 16, 256)
        for k in range(16):
            ar_ref[2 * k, 8:12, :] = gram[8 * k : 8 * k + 4]
            ar_ref[2 * k + 1, 8:12, :] = gram[8 * k + 4 : 8 * k + 8]
        ar_ref[:, 12:16, :] = jnp.zeros((PLANE, 4, 128), F32)
        last = ct_ref[PLANE - 1, 14:16, :]
        ar_ref[0, 12:14, :] = last[:, 0:128]
        ar_ref[0, 14:16, :] = last[:, 128:256]


def local_sums(x, psi, om):
    cells, times = x.shape
    block = cells // STEPS
    sketch, rank = psi.shape[0], om.shape[1]
    return pl.pallas_call(
        local_kernel,
        grid=(STEPS,),
        in_specs=[
            pl.BlockSpec((block, times), lambda i: (i, 0)),
            pl.BlockSpec((sketch, block), lambda i: (0, i)),
            pl.BlockSpec((times, rank), lambda i: (0, 0)),
        ],
        out_specs=[
            pl.BlockSpec((PLANE, 16, 128), lambda i: (0, 0, 0)),
            pl.BlockSpec((PLANE, 16, 256), lambda i: (0, 0, 0)),
            pl.BlockSpec((rank, block), lambda i: (0, i)),
        ],
        out_shape=[
            jax.ShapeDtypeStruct((PLANE, 16, 128), F32),
            jax.ShapeDtypeStruct((PLANE, 16, 256), F32),
            jax.ShapeDtypeStruct((rank, cells), F32),
        ],
        scratch_shapes=[pltpu.VMEM((sketch, times), F32), pltpu.VMEM((256, 256), F32)],
        compiler_params=pltpu.CompilerParams(
            dimension_semantics=("arbitrary",), vmem_limit_bytes=48 << 20
        ),
        name="local_sums",
    )(x, psi, om)


def place():
    s = lax.axis_index("space")
    return s // (ZS * XS), (s // XS) % ZS, s % XS, lax.axis_index("tm")


def plane_peer(q, z):
    return ((q // (XS * CS) * ZS + z) * XS + (q // CS) % XS, q % CS)


def ring_peer(index):
    index = lax.rem(index + 256, 256)
    return (index // CS, index % CS)


def comm_kernel(
    ar, ct, adj, sums, mine, halo,
    ar_in, ct_in, part, z_in, done, ct_part, ctz_in, edge,
    ar_send, ar_recv, ct_send, ct_recv, z_send, z_recv, g_send, g_recv, cz_send, cz_recv,
    h_send, h_recv,
):
    y, z, x, c = place()
    q = (y * XS + x) * CS + c
    me = ((y * ZS + z) * XS + x) * CS + c

    barrier = pltpu.get_barrier_semaphore()

    def greet(d, carry):
        pl.semaphore_signal(
            barrier, inc=1, device_id=plane_peer((q + d) % PLANE, z), device_id_type=MESH
        )
        return carry

    lax.fori_loop(1, PLANE, greet, 0)

    def z_peer(zz):
        return ((y * ZS + zz) * XS + x, c)

    for d in range(1, ZS):
        pl.semaphore_signal(barrier, inc=1, device_id=z_peer((z + d) % ZS), device_id_type=MESH)
    for d in (1, -1):
        pl.semaphore_signal(barrier, inc=1, device_id=ring_peer(me + d), device_id_type=MESH)
    pl.semaphore_wait(barrier, PLANE - 1 + ZS - 1 + 2)

    def ar_copy(to, slot_from, slot_to, send):
        return pltpu.make_async_remote_copy(
            src_ref=ar.at[slot_from], dst_ref=ar_in.at[slot_to],
            send_sem=ar_send.at[send], recv_sem=ar_recv.at[slot_to],
            device_id=to, device_id_type=MESH,
        )

    def ct_copy(to, slot_from, slot_to, send):
        return pltpu.make_async_remote_copy(
            src_ref=ct.at[slot_from], dst_ref=ct_in.at[slot_to],
            send_sem=ct_send.at[send], recv_sem=ct_recv.at[slot_to],
            device_id=to, device_id_type=MESH,
        )

    def z_copy(to, slot_to, send):
        return pltpu.make_async_remote_copy(
            src_ref=part, dst_ref=z_in.at[slot_to],
            send_sem=z_send.at[send], recv_sem=z_recv.at[slot_to],
            device_id=to, device_id_type=MESH,
        )

    def g_copy(to, slot_to, send):
        return pltpu.make_async_remote_copy(
            src_ref=done, dst_ref=sums.at[slot_to],
            send_sem=g_send.at[send], recv_sem=g_recv.at[slot_to],
            device_id=to, device_id_type=MESH,
        )

    def cz_copy(to, slot_from, slot_to, send):
        return pltpu.make_async_remote_copy(
            src_ref=ct_part.at[slot_from], dst_ref=ctz_in.at[slot_to],
            send_sem=cz_send.at[send], recv_sem=cz_recv.at[slot_to],
            device_id=to, device_id_type=MESH,
        )

    def h_copy(which):
        return pltpu.make_async_remote_copy(
            src_ref=edge.at[which], dst_ref=halo.at[which],
            send_sem=h_send.at[which], recv_sem=h_recv.at[which],
            device_id=ring_peer(me + (1 if which == 0 else -1)), device_id_type=MESH,
        )

    edge[0] = adj[7:8, :]
    edge[1] = adj[0:1, :]

    def loop(low, high, body):
        def step(d, carry):
            body(d)
            return carry

        lax.fori_loop(low, high, step, 0)

    loop(1, PLANE, lambda d: ar_copy(
        plane_peer((q + d) % PLANE, z), (q + d) % PLANE, q, d).start())
    loop(1, PLANE, lambda d: ct_copy(
        plane_peer((q + d) % PLANE, z), (q + d) % PLANE, q, d).start())
    h_copy(0).start()
    h_copy(1).start()
    ar_in[q] = ar[q]
    ct_in[q] = ct[q]
    loop(1, PLANE, lambda d: ar_copy(
        plane_peer((q + d) % PLANE, z), q, (q + d) % PLANE, d).wait_recv())
    part[...] = jnp.sum(ar_in[...], axis=0)

    for d in range(1, ZS):
        z_copy(z_peer((z + d) % ZS), z, d).start()
    z_in[z] = part[...]
    for d in range(1, ZS):
        z_copy(z_peer((z + d) % ZS), (z + d) % ZS, d).wait_recv()
    total = jnp.sum(z_in[...], axis=0)
    done[...] = total

    loop(1, PLANE, lambda d: g_copy(plane_peer((q + d) % PLANE, z), q, d).start())
    sums[q] = total

    loop(1, PLANE, lambda d: ct_copy(
        plane_peer((q + d) % PLANE, z), q, (q + d) % PLANE, d).wait_recv())
    ct_sum = jnp.sum(ct_in[...], axis=0)
    for zz in range(ZS):
        ct_part[zz] = ct_sum[2 * zz : 2 * zz + 2]
    for d in range(1, ZS):
        cz_copy(z_peer((z + d) % ZS), (z + d) % ZS, z, d).start()
    ctz_in[z] = ct_part[z]

    loop(1, PLANE, lambda d: g_copy(
        plane_peer((q + d) % PLANE, z), (q + d) % PLANE, d).wait_recv())
    for d in range(1, ZS):
        cz_copy(z_peer((z + d) % ZS), z, (z + d) % ZS, d).wait_recv()
    mine[...] = jnp.sum(ctz_in[...], axis=0)

    h_copy(0).wait_recv()
    h_copy(1).wait_recv()
    h_copy(0).wait_send()
    h_copy(1).wait_send()
    loop(1, PLANE, lambda d: ar_copy(plane_peer(q, z), q, q, d).wait_send())
    loop(1, PLANE, lambda d: ct_copy(plane_peer(q, z), q, q, d).wait_send())
    loop(1, PLANE, lambda d: g_copy(plane_peer(q, z), q, d).wait_send())
    for d in range(1, ZS):
        z_copy(z_peer(z), z, d).wait_send()
        cz_copy(z_peer(z), z, z, d).wait_send()


def exchange(ar, ct, adj):
    vmem = pl.BlockSpec(memory_space=pltpu.VMEM)
    dma = pltpu.SemaphoreType.DMA
    width = adj.shape[1]
    return pl.pallas_call(
        comm_kernel,
        in_specs=[vmem] * 3,
        out_specs=[vmem] * 3,
        out_shape=[
            jax.ShapeDtypeStruct((PLANE, 16, 128), F32),
            jax.ShapeDtypeStruct((2, 256), F32),
            jax.ShapeDtypeStruct((2, 1, width), F32),
        ],
        scratch_shapes=[
            pltpu.VMEM((PLANE, 16, 128), F32),
            pltpu.VMEM((PLANE, 16, 256), F32),
            pltpu.VMEM((16, 128), F32),
            pltpu.VMEM((ZS, 16, 128), F32),
            pltpu.VMEM((16, 128), F32),
            pltpu.VMEM((ZS, 2, 256), F32),
            pltpu.VMEM((ZS, 2, 256), F32),
            pltpu.VMEM((2, 1, width), F32),
            dma((PLANE,)), dma((PLANE,)), dma((PLANE,)), dma((PLANE,)),
            dma((ZS,)), dma((ZS,)), dma((PLANE,)), dma((PLANE,)),
            dma((ZS,)), dma((ZS,)), dma((2,)), dma((2,)),
        ],
        compiler_params=pltpu.CompilerParams(collective_id=0, has_side_effects=True),
        name="exchange",
    )(ar, ct, adj)


def lane(a, k):
    return jnp.broadcast_to(a[:, k : k + 1], (8, 128))


def sub(a, k):
    return jnp.broadcast_to(a[k : k + 1, :], (8, 128))


def panel_steps(panel, k0, in_place):
    subs, lanes = iota((8, 128), 0), iota((8, 128), 1)
    cols = [lane(panel, k0 + j) for j in range(8)]
    upper = jnp.zeros((8, 128), F32)
    for i in range(8):
        here = subs == i
        pivot = sub(cols[i], i)
        inverse = 1.0 / pivot
        if in_place:
            panel = jnp.where(lanes == k0 + i, jnp.where(here, 1.0, 0.0), panel)
        else:
            upper = jnp.where(here & (lanes >= k0 + i), panel * lax.rsqrt(pivot), upper)
        row = sub(panel, i) * inverse
        panel = jnp.where(here, row, panel - cols[i] * row)
        for j in range(i + 1, 8):
            entry = sub(cols[j], i) * inverse
            cols[j] = jnp.where(here, entry, cols[j] - cols[i] * entry)
    return panel, upper


def upper_factor(rows):
    rows = list(rows)
    out = []
    for k in range(16):
        k0 = 8 * k
        panel, upper = panel_steps(rows[k], k0, False)
        out.append(upper)
        pieces = [sub(panel, j) for j in range(8)]
        for b in range(k + 1, 16):
            update = lane(rows[b], k0) * pieces[0]
            for j in range(1, 8):
                update = update + lane(rows[b], k0 + j) * pieces[j]
            rows[b] = rows[b] - update
    return out


def solve_rows(rows, right):
    rows = list(rows)
    lanes = iota((8, 128), 1)
    for k in range(16):
        k0 = 8 * k
        inside = (lanes >= k0) & (lanes < k0 + 8)
        panel, _ = panel_steps(rows[k], k0, True)
        panel = jnp.where(inside, -panel, panel)
        pieces = [sub(panel, j) for j in range(8)]
        for b in range(k + 1, 17):
            old = right if b == 16 else rows[b]
            update = lane(old, k0) * pieces[0]
            for j in range(1, 8):
                update = update + lane(old, k0 + j) * pieces[j]
            new = jnp.where(inside, 0.0, old) - update
            if b == 16:
                right = new
            else:
                rows[b] = new
    return right


def shifted(field, low, high):
    up = jnp.concatenate([low, field[0:7]], axis=0)
    down = jnp.concatenate([field[1:8], high], axis=0)
    nothing = jnp.zeros((8, 1), F32)
    left = jnp.concatenate([nothing, field[:, :-1]], axis=1)
    right = jnp.concatenate([field[:, 1:], nothing], axis=1)
    return up + down + left + right - 4.0 * field


def masked_halo(halo, me):
    low = jnp.where(me == 0, 0.0, halo[0])
    high = jnp.where(me == 255, 0.0, halo[1])
    return low, high


def solve_kernel(
    sums, mine, halo, yt_hbm, adj, species, rates, me_ref, adj_out, growth_out, t_out, yt, sem
):
    fetch = pltpu.make_async_copy(yt_hbm, yt, sem)
    fetch.start()
    raw = sums[:, 0:8, :].reshape(256, 128)
    gram = [
        jnp.concatenate([sums[2 * k, 8:12, :], sums[2 * k + 1, 8:12, :]], axis=0)
        for k in range(16)
    ]
    last = jnp.concatenate([sums[0, 12:14, :], sums[0, 14:16, :]], axis=1)
    right = jnp.concatenate([mine[...], last, jnp.zeros((4, 256), F32)], axis=0)
    right = jnp.dot(right, raw, precision=HIGH)
    normal = lax.dot_general(raw, raw, (((0,), (0,)), ((), ())), precision=HIGH)
    upper = upper_factor(gram)
    solved = solve_rows([normal[8 * k : 8 * k + 8] for k in range(16)], right)
    factor = jnp.concatenate(upper, axis=0)
    t_out[...] = lax.dot_general(
        solved, factor, (((1,), (1,)), ((), ())), precision=HIGH
    ) * (2097152.0 ** -0.5)
    columns = jnp.concatenate([solved] * 16, axis=0).T

    kinds = species[...]
    coupling = jnp.zeros(kinds.shape, F32)
    for kind in range(4):
        coupling = jnp.where(kinds == kind, rates[kind], coupling)

    fetch.wait()

    def state(j):
        weights = jnp.broadcast_to(columns[:, j : j + 1], (128, 128))
        tiles = []
        for b in range(8):
            parts = []
            for xx in range(8):
                at = xx * 1024 + b * 128
                parts.append(jnp.sum(yt[:, at : at + 128] * weights, axis=0, keepdims=True))
            tiles.append(jnp.concatenate(parts, axis=0))
        return jnp.concatenate(tiles, axis=1)

    first, second = state(3), state(2)
    field = adj[...]
    low, high = masked_halo(halo, me_ref[0])
    adj_out[...] = (
        field
        + DIFFUSION * shifted(field, low, high)
        + STEP_SIZE * coupling * (1.0 - 3.0 * first * first) * field
    )
    growth_out[...] = STEP_SIZE * coupling * (1.0 - 3.0 * second * second)


def solve(sums, mine, halo, yt, adj, species, rates, me):
    vmem = pl.BlockSpec(memory_space=pltpu.VMEM)
    smem = pl.BlockSpec(memory_space=pltpu.SMEM)
    return pl.pallas_call(
        solve_kernel,
        in_specs=[vmem, vmem, vmem, pl.BlockSpec(memory_space=pl.ANY), vmem, vmem, smem, smem],
        out_specs=[vmem] * 3,
        out_shape=[
            jax.ShapeDtypeStruct(adj.shape, F32),
            jax.ShapeDtypeStruct(adj.shape, F32),
            jax.ShapeDtypeStruct((8, 128), F32),
        ],
        scratch_shapes=[pltpu.VMEM(yt.shape, F32), pltpu.SemaphoreType.DMA],
        compiler_params=pltpu.CompilerParams(vmem_limit_bytes=48 << 20),
        name="solve",
    )(sums, mine, halo, yt, adj, species, rates, me)


def last_kernel(adj, growth, out, edge, halo, send, recv):
    y, z, x, c = place()
    me = ((y * ZS + z) * XS + x) * CS + c
    barrier = pltpu.get_barrier_semaphore()
    for d in (1, -1):
        pl.semaphore_signal(barrier, inc=1, device_id=ring_peer(me + d), device_id_type=MESH)
    edge[0] = adj[7:8, :]
    edge[1] = adj[0:1, :]
    pl.semaphore_wait(barrier, 2)

    def copy(which):
        return pltpu.make_async_remote_copy(
            src_ref=edge.at[which], dst_ref=halo.at[which],
            send_sem=send.at[which], recv_sem=recv.at[which],
            device_id=ring_peer(me + (1 if which == 0 else -1)), device_id_type=MESH,
        )

    copy(0).start()
    copy(1).start()
    field = adj[...]
    copy(0).wait()
    copy(1).wait()
    low, high = masked_halo(halo, me)
    out[...] = field + DIFFUSION * shifted(field, low, high) + growth[...] * field


def last_step(adj, growth):
    vmem = pl.BlockSpec(memory_space=pltpu.VMEM)
    dma = pltpu.SemaphoreType.DMA
    return pl.pallas_call(
        last_kernel,
        in_specs=[vmem] * 2,
        out_specs=vmem,
        out_shape=jax.ShapeDtypeStruct(adj.shape, F32),
        scratch_shapes=[
            pltpu.VMEM((2, 1, adj.shape[1]), F32),
            pltpu.VMEM((2, 1, adj.shape[1]), F32),
            dma((2,)), dma((2,)),
        ],
        compiler_params=pltpu.CompilerParams(collective_id=1, has_side_effects=True),
        name="last_step",
    )(adj, growth)


def shards(snapshots, range_test, test_rows, species, reaction_rates, adjoint_end):
    ar, ct, yt = local_sums(snapshots, test_rows, range_test)
    sums, mine, halo = exchange(ar, ct, adjoint_end)
    me = (lax.axis_index("space") * CS + lax.axis_index("tm")).astype(jnp.int32).reshape(1)
    adjoint, growth, factors = solve(
        sums, mine, halo, yt, adjoint_end, species, reaction_rates, me
    )
    adjoint = last_step(adjoint, growth)
    return adjoint, factors[0:2].T


def solution(mesh):
    cells = ("space", "tm")
    in_specs = (P(cells, None), P(), P(None, cells), P(cells, None), P(), P(cells, None))
    out_specs = (P(cells, None), P(None, cells))
    return jax.shard_map(
        shards, mesh=mesh, in_specs=in_specs, out_specs=out_specs, check_vma=False
    )
```

time: 410 us -> 77.7 us (0.19); the launches traced: 405 us -> 77.1 us
  waiting for transfers between devices: 253 us -> 0 us
  Pallas kernels: 0 us -> 64.4 us
  other arithmetic: 48.4 us -> 0 us
  blocking collectives: 39.1 us -> 0 us
  matrix products: 35.5 us -> 0 us
  between operations: 14.4 us -> 0.73 us
  starting transfers between devices: 12.6 us -> 0 us
  local copies, waits for them, and re-layouts: 2.22 us -> 12 us
    psum x1 -> x0, waiting for transfers between devices: 252 us -> none  [together(): running = lax.psum(vector, axis)]
    pallas_call x0 -> x4, Pallas kernels: none -> 64.4 us  [the longest x1 32.8 us: exchange(): pl.pallas_call(comm_kernel, in_specs=[vmem] * 3, out_specs=[vmem] * 3, ou...]
    another operation x10 -> x0, other arithmetic: 45.9 us -> none  [the longest x3 12.6 us: shards(): normal_factor = jnp.linalg.cholesky(normal_matrix)]
    psum x4 -> x0, blocking collectives: 39.1 us -> none  [from_root(): value = lax.psum(value, axis)]
    dot_general x7 -> x0, matrix products: 25.3 us -> none  [the longest x1 6.91 us: shards(): lax.dot_general(range_part, range_part, contract_rows, precision=high)]
    ppermute x4 -> x0, starting transfers between devices: 12.6 us -> none  [the longest x2 7.36 us: with_halo(): lax.ppermute(lax.slice_in_dim(block, 0, width, axis=dim), axis, backward)]
    unnamed x16 -> x27, local copies, waits for them, and re-layouts: 0.9 us -> 11.4 us
    another operation x4 -> x0, matrix products: 10.1 us -> none  [the longest x1 7.92 us: shards(): jax.scipy.linalg.solve_triangular(lower_factor, range_part.T, lower=True)]
  transfers between devices with their start and end apart: 5 -> 0, of which waited for: 2 -> 0; matrix products, arithmetic and copies ran while one was open for 16% -> 0% of each run, Pallas kernels for 0% -> 0%
where the time goes in v1:
time: 77.7 us; the launch traced here: 77.1 us
  Pallas kernels  64.4 us (83%)
  local copies, waits for them, and re-layouts  12 us (15%)
    pallas_call x1, Pallas kernels, exchange(): pl.pallas_call(comm_kernel, in_specs=[vmem] * 3, out_specs=[vmem] * 3, ou...  32.8 us
    pallas_call x1, Pallas kernels, local_sums(): pl.pallas_call(local_kernel, grid=(STEPS,), in_specs=[pl.BlockSpec((block...  12.5 us
    unnamed x27, local copies, waits for them, and re-layouts  11.4 us
    pallas_call x1, Pallas kernels, solve(): pl.pallas_call(solve_kernel, in_specs=[vmem, vmem, vmem, pl.BlockSpec(mem...  11 us
    pallas_call x1, Pallas kernels, last_step(): pl.pallas_call(last_kernel, in_specs=[vmem] * 2, out_specs=vmem, out_shap...  8.04 us

profile of v1, /device:TPU:1, one launch (start us, length us, event | category | flops | bytes accessed | tf_op | source)
XLA Modules:
  0.0 77.1 jit_solution(3904223166314444577)
XLA Ops:
  0.6 0.0 copy-start.5
  0.6 0.9 %copy-done.5 = bf16[512,128]{1,0:T(8,128)(2,1)S(1)} copy-done((bf16[512,128]{1,0:T(8,128)(2,1)S(1)}, bf16[512,128]{1,0:T(8,128)(2,1)}, u32[]{:S(2)}) %copy-start.5) | copy-done | bytes 131096
  1.5 0.0 copy-start.6
  1.5 12.5 %local_sums.1 = (f32[32,16,128]{2,1,0:T(8,128)S(1)}, f32[32,16,256]{2,1,0:T(8,128)S(1)}, f32[128,8192]{1,0:T(8,128)S(1)}) custom-call(bf16[8192,512]{1,0:T(8,128)(2,1)} %x_ref.1, bf16[256,8192]{1,0:T(8,128)(2,1)} %psi_ref.1, bf16[512,128]{1,0:T(8,128)(2,1)S(1)} %copy-done.5), custom_call_target="tpu_custom_call" | custom-call | tf_op jit(solution)/shard_map/local_sums/pallas_call | solution.py:85
  14.1 0.0 copy-start
  14.1 1.9 %copy-done = f32[128,8192]{1,0:T(8,128)} copy-done((f32[128,8192]{1,0:T(8,128)}, f32[128,8192]{1,0:T(8,128)S(1)}, u32[]{:S(2)}) %copy-start) | copy-done | bytes 4194328
  16.0 0.8 %copy-done.2 = f32[32,16,256]{2,1,0:T(8,128)} copy-done((f32[32,16,256]{2,1,0:T(8,128)}, f32[32,16,256]{2,1,0:T(8,128)S(1)}, u32[]{:S(2)}) %copy-start.2) | copy-done | bytes 524312
  16.8 0.7 copy-done.4
  17.5 32.8 %exchange.1 = (f32[32,16,128]{2,1,0:T(8,128)}, f32[2,256]{1,0:T(2,128)}, f32[2,1,1024]{2,1,0:T(1,128)}) custom-call(f32[32,16,128]{2,1,0:T(8,128)} %copy-done.4, f32[32,16,256]{2,1,0:T(8,128)} %copy-done.2, f32[8,1024]{1,0:T(8,128)} %adj.3), custom_call_target="tpu_custom_call" | custom-call | tf_op jit(solution)/shard_map/exchange/pallas_call | solution.py:260
  50.4 0.0 copy-done.6
  50.4 0.0 copy-done.7
  50.4 0.0 copy-done.12
  50.4 0.0 copy-start.1
  50.4 2.2 %copy-done.1 = f32[128,8192]{1,0:T(8,128)S(1)} copy-done((f32[128,8192]{1,0:T(8,128)S(1)}, f32[128,8192]{1,0:T(8,128)}, u32[]{:S(2)}) %copy-start.1) | copy-done | bytes 4194328
  52.6 0.9 %copy-done.3 = f32[32,16,128]{2,1,0:T(8,128)S(1)} copy-done((f32[32,16,128]{2,1,0:T(8,128)S(1)}, f32[32,16,128]{2,1,0:T(8,128)}, u32[]{:S(2)}) %copy-start.3) | copy-done | bytes 262168
  53.6 0.7 copy-done.10
  54.3 0.7 copy-done.11
  54.9 11.0 %solve.1 = (f32[8,1024]{1,0:T(8,128)S(1)}, f32[8,1024]{1,0:T(8,128)S(1)}, f32[8,128]{1,0:T(8,128)S(1)}) custom-call(f32[32,16,128]{2,1,0:T(8,128)S(1)} %copy-done.3, f32[2,256]{1,0:T(2,128)S(1)} %copy-done.11, f32[2,1,1024]{2,1,0:T(1,128)S(1)} %copy-done.10, f32[128,8192]{1,0:T(8,128)S(1)} %copy-done.1, f32[8,1024]{1,0:T(8,128)S(1)} %copy-done.6, ...), custom_call_target="tpu_custom_call" | custom-call | tf_op jit(solution)/shard_map/solve/pallas_call | solution.py:422
  65.9 0.0 copy-start.8
  65.9 0.6 copy-done.8
  66.5 0.6 copy-done.9
  67.1 8.0 %last_step.1 = f32[8,1024]{1,0:T(8,128)} custom-call(f32[8,1024]{1,0:T(8,128)} %copy-done.8, f32[8,1024]{1,0:T(8,128)} %copy-done.9), custom_call_target="tpu_custom_call" | custom-call | tf_op jit(solution)/shard_map/last_step/pallas_call | solution.py:466
  75.2 0.6 slice_bitcast_fusion
  75.7 1.4 %copy.9 = f32[8,1024]{1,0:T(8,128)} copy(f32[8,1024]{1,0:T(8,128)} %last_step.1) | data formatting | bytes 65536
  (8 shorter events, 0.0 us)
Async XLA Ops:
  0.6 0.9 %copy-start.5 = (bf16[512,128]{1,0:T(8,128)(2,1)S(1)}, bf16[512,128]{1,0:T(8,128)(2,1)}, u32[]{:S(2)}) copy-start(bf16[512,128]{1,0:T(8,128)(2,1)} %om_ref.1) | copy-start | bytes 393220
  1.5 48.8 %copy-start.6 = (f32[8,1024]{1,0:T(8,128)S(1)}, f32[8,1024]{1,0:T(8,128)}, u32[]{:S(2)}) copy-start(f32[8,1024]{1,0:T(8,128)} %adj.3) | copy-start | bytes 98308
  1.5 48.9 %copy-start.7 = (s32[8,1024]{1,0:T(8,128)S(1)}, s32[8,1024]{1,0:T(8,128)}, u32[]{:S(2)}) copy-start(s32[8,1024]{1,0:T(8,128)} %species.1) | copy-start | bytes 98308
  1.5 48.9 %copy-start.12 = (f32[4]{0:T(128)S(1)}, f32[4]{0:T(128)}, u32[]{:S(2)}) copy-start(f32[4]{0:T(128)} %rates.1) | copy-start | bytes 52
  14.1 2.0 %copy-start = (f32[128,8192]{1,0:T(8,128)}, f32[128,8192]{1,0:T(8,128)S(1)}, u32[]{:S(2)}) copy-start(f32[128,8192]{1,0:T(8,128)S(1)} %get-tuple-element.16.yt_hbm) | copy-start | bytes 12582916
  16.0 0.8 %copy-start.2 = (f32[32,16,256]{2,1,0:T(8,128)}, f32[32,16,256]{2,1,0:T(8,128)S(1)}, u32[]{:S(2)}) copy-start(f32[32,16,256]{2,1,0:T(8,128)S(1)} %get-tuple-element.12.ct) | copy-start | bytes 1572868
  16.8 0.7 copy-start.4
  50.4 2.2 %copy-start.1 = (f32[128,8192]{1,0:T(8,128)S(1)}, f32[128,8192]{1,0:T(8,128)}, u32[]{:S(2)}) copy-start(f32[128,8192]{1,0:T(8,128)} %copy-done) | copy-start | bytes 12582916
  52.6 0.9 %copy-start.3 = (f32[32,16,128]{2,1,0:T(8,128)S(1)}, f32[32,16,128]{2,1,0:T(8,128)}, u32[]{:S(2)}) copy-start(f32[32,16,128]{2,1,0:T(8,128)} %get-tuple-element.13.sums) | copy-start | bytes 786436
  53.6 0.7 copy-start.10
  54.2 0.7 copy-start.11
  65.9 0.6 copy-start.8
  66.5 0.6 copy-start.9

commit v2 on v0

v2 whole, which is shorter than its diff:
```python
import functools

import jax
import jax.numpy as jnp
from jax import lax
from jax.experimental import pallas as pl
from jax.experimental.pallas import tpu as pltpu
from jax.sharding import PartitionSpec as P

DIFFUSION = 0.2
STEP_SIZE = 0.05
MESH = pl.DeviceIdType.MESH
HIGH = lax.Precision.HIGHEST
F32 = jnp.float32
BF16 = jnp.bfloat16

YS, ZS, XS, CS = 4, 8, 4, 2
PLANE = YS * XS * CS
STEPS = 8
WIDTH = 1024


def iota(shape, dim):
    return lax.broadcasted_iota(jnp.int32, shape, dim)


def place():
    s = lax.axis_index("space")
    return s // (ZS * XS), (s // XS) % ZS, s % XS, lax.axis_index("tm")


def plane_peer(q, z):
    return ((q // (XS * CS) * ZS + z) * XS + (q // CS) % XS, q % CS)


def ring_peer(index):
    index = lax.rem(index + 256, 256)
    return (index // CS, index % CS)


def lane(a, k):
    return jnp.broadcast_to(a[:, k : k + 1], (8, 128))


def sub(a, k):
    return jnp.broadcast_to(a[k : k + 1, :], (8, 128))


def panel_steps(panel, k0, in_place):
    subs, lanes = iota((8, 128), 0), iota((8, 128), 1)
    cols = [lane(panel, k0 + j) for j in range(8)]
    upper = jnp.zeros((8, 128), F32)
    for i in range(8):
        here = subs == i
        pivot = sub(cols[i], i)
        inverse = 1.0 / pivot
        if in_place:
            panel = jnp.where(lanes == k0 + i, jnp.where(here, 1.0, 0.0), panel)
        else:
            upper = jnp.where(here & (lanes >= k0 + i), panel * lax.rsqrt(pivot), upper)
        row = sub(panel, i) * inverse
        panel = jnp.where(here, row, panel - cols[i] * row)
        for j in range(i + 1, 8):
            entry = sub(cols[j], i) * inverse
            cols[j] = jnp.where(here, entry, cols[j] - cols[i] * entry)
    return panel, upper


def upper_factor(rows):
    rows = list(rows)
    out = []
    for k in range(16):
        k0 = 8 * k
        panel, upper = panel_steps(rows[k], k0, False)
        out.append(upper)
        pieces = [sub(panel, j) for j in range(8)]
        for b in range(k + 1, 16):
            update = lane(rows[b], k0) * pieces[0]
            for j in range(1, 8):
                update = update + lane(rows[b], k0 + j) * pieces[j]
            rows[b] = rows[b] - update
    return out


def solve_rows(rows, right):
    rows = list(rows)
    lanes = iota((8, 128), 1)
    for k in range(16):
        k0 = 8 * k
        inside = (lanes >= k0) & (lanes < k0 + 8)
        panel, _ = panel_steps(rows[k], k0, True)
        panel = jnp.where(inside, -panel, panel)
        pieces = [sub(panel, j) for j in range(8)]
        for b in range(k + 1, 17):
            old = right if b == 16 else rows[b]
            update = lane(old, k0) * pieces[0]
            for j in range(1, 8):
                update = update + lane(old, k0 + j) * pieces[j]
            new = jnp.where(inside, 0.0, old) - update
            if b == 16:
                right = new
            else:
                rows[b] = new
    return right


def sideways(field):
    nothing = jnp.zeros((field.shape[0], 1), F32)
    left = jnp.concatenate([nothing, field[:, :-1]], axis=1)
    right = jnp.concatenate([field[:, 1:], nothing], axis=1)
    return left + right - 4.0 * field


def coupling_of(kinds, rates):
    coupling = jnp.zeros(kinds.shape, F32)
    for kind in range(4):
        coupling = jnp.where(kinds == kind, rates[kind], coupling)
    return coupling


def loop(low, high, body):
    def step(d, carry):
        body(d)
        return carry

    lax.fori_loop(low, high, step, 0)


def whole_kernel(
    x_hbm, om_hbm, psi_hbm, spec_hbm, rates, adj_hbm,
    adj_out, t_out,
    xb, psib, omb, spec, adj, yt, c_acc, k_acc,
    ar, ct, ar_in, ct_in, part, z_in, done, sums, ct_part, ctz_in, edge, halo, halo_y,
    x_sem, psi_sem, small_sem,
    ar_send, ar_recv, ct_send, ct_recv, z_send, z_recv, g_send, g_recv, cz_send, cz_recv,
    h_send, h_recv, y_send, y_recv,
):
    y, z, x, c = place()
    q = (y * XS + x) * CS + c
    me = ((y * ZS + z) * XS + x) * CS + c

    def x_copy(k):
        return pltpu.make_async_copy(
            x_hbm.at[pl.ds(k * WIDTH, WIDTH), :], xb.at[k], x_sem.at[k])

    def psi_copy(k):
        return pltpu.make_async_copy(
            psi_hbm.at[:, pl.ds(k * WIDTH, WIDTH)], psib.at[k], psi_sem.at[k])

    om_copy = pltpu.make_async_copy(om_hbm, omb, small_sem.at[0])
    spec_copy = pltpu.make_async_copy(spec_hbm, spec, small_sem.at[1])
    adj_copy = pltpu.make_async_copy(adj_hbm, adj, small_sem.at[2])
    om_copy.start()
    for i in range(STEPS):
        x_copy((i + 7) % STEPS).start()
        psi_copy((i + 7) % STEPS).start()
        if i == 1:
            spec_copy.start()
            adj_copy.start()

    barrier = pltpu.get_barrier_semaphore()
    loop(1, PLANE, lambda d: pl.semaphore_signal(
        barrier, inc=1, device_id=plane_peer((q + d) % PLANE, z), device_id_type=MESH))

    def z_peer(zz):
        return ((y * ZS + zz) * XS + x, c)

    for d in range(1, ZS):
        pl.semaphore_signal(barrier, inc=1, device_id=z_peer((z + d) % ZS), device_id_type=MESH)
    for d in (1, -1):
        pl.semaphore_signal(barrier, inc=1, device_id=ring_peer(me + d), device_id_type=MESH)

    def ar_copy(to, slot_from, slot_to, send):
        return pltpu.make_async_remote_copy(
            src_ref=ar.at[slot_from], dst_ref=ar_in.at[slot_to],
            send_sem=ar_send.at[send], recv_sem=ar_recv.at[slot_to],
            device_id=to, device_id_type=MESH)

    def ct_copy(to, slot_from, slot_to, send):
        return pltpu.make_async_remote_copy(
            src_ref=ct.at[slot_from], dst_ref=ct_in.at[slot_to],
            send_sem=ct_send.at[send], recv_sem=ct_recv.at[slot_to],
            device_id=to, device_id_type=MESH)

    def z_copy(to, slot_to, send):
        return pltpu.make_async_remote_copy(
            src_ref=part, dst_ref=z_in.at[slot_to],
            send_sem=z_send.at[send], recv_sem=z_recv.at[slot_to],
            device_id=to, device_id_type=MESH)

    def g_copy(to, slot_to, send):
        return pltpu.make_async_remote_copy(
            src_ref=done, dst_ref=sums.at[slot_to],
            send_sem=g_send.at[send], recv_sem=g_recv.at[slot_to],
            device_id=to, device_id_type=MESH)

    def cz_copy(to, slot_from, slot_to, send):
        return pltpu.make_async_remote_copy(
            src_ref=ct_part.at[slot_from], dst_ref=ctz_in.at[slot_to],
            send_sem=cz_send.at[send], recv_sem=cz_recv.at[slot_to],
            device_id=to, device_id_type=MESH)

    def h_copy(which):
        return pltpu.make_async_remote_copy(
            src_ref=edge.at[which], dst_ref=halo.at[which],
            send_sem=h_send.at[which], recv_sem=h_recv.at[which],
            device_id=ring_peer(me + (1 if which == 0 else -1)), device_id_type=MESH)

    def y_copy(which):
        return pltpu.make_async_remote_copy(
            src_ref=yt.at[7 if which == 0 else 0], dst_ref=halo_y.at[which],
            send_sem=y_send.at[which], recv_sem=y_recv.at[which],
            device_id=ring_peer(me + (1 if which == 0 else -1)), device_id_type=MESH)

    om_copy.wait()
    c_acc[...] = jnp.zeros_like(c_acc)
    k_acc[...] = jnp.zeros_like(k_acc)

    def block(i):
        k = (i + 7) % STEPS
        x_copy(k).wait()
        psi_copy(k).wait()
        xs = xb[k]
        ys = jnp.dot(xs, omb[...], preferred_element_type=F32)
        ys_t = ys.T
        yt[k] = ys_t
        hi = ys.astype(BF16)
        lo = (ys - hi.astype(F32)).astype(BF16)
        hi_t = ys_t.astype(BF16)
        lo_t = (ys_t - hi_t.astype(F32)).astype(BF16)
        wide = jnp.concatenate([hi, lo], axis=1)
        wide_t = jnp.concatenate([hi_t, lo_t], axis=0)
        k_acc[...] += jnp.dot(wide_t, wide, preferred_element_type=F32)
        c_acc[...] += jnp.dot(psib[k], xs, preferred_element_type=F32)

    loop(0, 2, block)
    spec_copy.wait()
    adj_copy.wait()
    coupling = coupling_of(spec[...], rates)
    edge[0, 0:1] = adj[7:8, :]
    edge[0, 1:2] = adj[6:7, :]
    edge[0, 2:3] = coupling[7:8, :]
    edge[0, 3:4] = coupling[7:8, :]
    edge[1, 0:1] = adj[0:1, :]
    edge[1, 1:2] = adj[1:2, :]
    edge[1, 2:3] = coupling[0:1, :]
    edge[1, 3:4] = coupling[0:1, :]
    pl.semaphore_wait(barrier, PLANE - 1 + ZS - 1 + 2)
    for which in range(2):
        y_copy(which).start()
        h_copy(which).start()
    loop(2, STEPS, block)

    r = 128
    gram = k_acc[0:r, 0:r] + k_acc[0:r, r:] + k_acc[r:, 0:r] + k_acc[r:, r:]
    om_f = omb[...]
    c_all = c_acc[...]
    c_1 = c_all.astype(BF16)
    rest = c_all - c_1.astype(F32)
    c_2 = rest.astype(BF16)
    c_3 = (rest - c_2.astype(F32)).astype(BF16)
    raw = (
        jnp.dot(c_3, om_f, preferred_element_type=F32)
        + jnp.dot(c_2, om_f, preferred_element_type=F32)
        + jnp.dot(c_1, om_f, preferred_element_type=F32)
    )
    ar[:, 0:8, :] = raw.reshape(PLANE, 8, r)
    for k in range(16):
        ar[2 * k, 8:12, :] = gram[8 * k : 8 * k + 4]
        ar[2 * k + 1, 8:12, :] = gram[8 * k + 4 : 8 * k + 8]
    row = iota((r, r), 0)
    source = ((row >> 1) & 7) * 16 + ((row >> 5) & 3) * 4 + ((row >> 4) & 1) * 2 + (row & 1)
    perm = jnp.where(iota((r, r), 1) == source, 1.0, 0.0).astype(F32)

    def turned(y_at):
        piece = lax.dot_general(
            perm, c_acc[:, y_at * r : (y_at + 1) * r], (((1,), (1,)), ((), ())),
            precision=HIGH, preferred_element_type=F32)
        ct[8 * y_at : 8 * y_at + 8] = piece.reshape(8, 16, 256)

    turned(YS - 1)
    ar[:, 12:16, :] = jnp.zeros((PLANE, 4, r), F32)
    ends = ct[PLANE - 1, 14:16, :]
    ar[0, 12:14, :] = ends[:, 0:128]
    ar[0, 14:16, :] = ends[:, 128:256]

    loop(1, PLANE, lambda d: ar_copy(
        plane_peer((q + d) % PLANE, z), (q + d) % PLANE, q, d).start())
    ar_in[q] = ar[q]
    for y_at in range(YS - 1):
        turned(y_at)
    ct_in[q] = ct[q]
    loop(1, PLANE, lambda d: ar_copy(
        plane_peer((q + d) % PLANE, z), q, (q + d) % PLANE, d).wait_recv())
    part[...] = jnp.sum(ar_in[...], axis=0)

    for d in range(1, ZS):
        z_copy(z_peer((z + d) % ZS), z, d).start()
    loop(1, PLANE, lambda d: ct_copy(
        plane_peer((q + d) % PLANE, z), (q + d) % PLANE, q, d).start())
    z_in[z] = part[...]
    for d in range(1, ZS):
        z_copy(z_peer((z + d) % ZS), (z + d) % ZS, d).wait_recv()
    total = jnp.sum(z_in[...], axis=0)
    done[...] = total

    loop(1, PLANE, lambda d: g_copy(plane_peer((q + d) % PLANE, z), q, d).start())
    sums[q] = total

    loop(1, PLANE, lambda d: ct_copy(
        plane_peer((q + d) % PLANE, z), q, (q + d) % PLANE, d).wait_recv())
    ct_sum = jnp.sum(ct_in[...], axis=0)
    for zz in range(ZS):
        ct_part[zz] = ct_sum[2 * zz : 2 * zz + 2]
    for d in range(1, ZS):
        cz_copy(z_peer((z + d) % ZS), (z + d) % ZS, z, d).start()
    ctz_in[z] = ct_part[z]

    loop(1, PLANE, lambda d: g_copy(
        plane_peer((q + d) % PLANE, z), (q + d) % PLANE, d).wait_recv())
    for d in range(1, ZS):
        cz_copy(z_peer((z + d) % ZS), z, (z + d) % ZS, d).wait_recv()
    mine = jnp.sum(ctz_in[...], axis=0)

    raw = sums[:, 0:8, :].reshape(256, r)
    gram_rows = [
        jnp.concatenate([sums[2 * k, 8:12, :], sums[2 * k + 1, 8:12, :]], axis=0)
        for k in range(16)
    ]
    last = jnp.concatenate([sums[0, 12:14, :], sums[0, 14:16, :]], axis=1)
    right = jnp.concatenate([mine, last, jnp.zeros((4, 256), F32)], axis=0)
    right = jnp.dot(right, raw, precision=HIGH)
    normal = lax.dot_general(raw, raw, (((0,), (0,)), ((), ())), precision=HIGH)
    upper = upper_factor(gram_rows)
    solved = solve_rows([normal[8 * k : 8 * k + 8] for k in range(16)], right)
    factor = jnp.concatenate(upper, axis=0)
    times = lax.dot_general(
        solved, factor, (((1,), (1,)), ((), ())), precision=HIGH
    ) * (2097152.0 ** -0.5)
    t_out[...] = times[0:2]
    columns = jnp.concatenate([solved] * 16, axis=0).T

    def state(blocks, j):
        weights = jnp.broadcast_to(columns[:, j : j + 1], (r, r))
        tiles = []
        for b in range(8):
            tiles.append(jnp.concatenate([
                jnp.sum(get(b * r) * weights, axis=0, keepdims=True) for get in blocks
            ], axis=0))
        return jnp.concatenate(tiles, axis=1)

    own = [functools.partial(lambda k, at: yt[k, :, at : at + r], k) for k in range(8)]
    y_copy(0).wait_recv()
    y_copy(1).wait_recv()
    h_copy(0).wait_recv()
    h_copy(1).wait_recv()
    outer = [functools.partial(lambda k, at: halo_y[k, :, at : at + r], k) for k in range(2)]
    first, second, edges = state(own, 3), state(own, 2), state(outer, 3)

    coupling = STEP_SIZE * coupling_of(spec[...], rates)
    field = adj[...]
    near = jnp.concatenate([halo[0, 0:1], halo[1, 0:1]], axis=0)
    far = jnp.concatenate([halo[0, 1:2], halo[1, 1:2]], axis=0)
    rate = jnp.concatenate([halo[0, 2:3], halo[1, 2:3]], axis=0) * STEP_SIZE
    inner = jnp.concatenate([field[0:1], field[7:8]], axis=0)
    side = iota((2, WIDTH), 0)
    absent = ((side == 0) & (me == 0)) | ((side == 1) & (me == 255))
    near = jnp.where(absent, 0.0, near)
    near_next = (
        near + DIFFUSION * (far + inner + sideways(near))
        + rate * (1.0 - 3.0 * edges * edges) * near
    )
    near_next = jnp.where(absent, 0.0, near_next)

    def advance(field, low, high, state):
        up = jnp.concatenate([low, field[0:7]], axis=0)
        down = jnp.concatenate([field[1:8], high], axis=0)
        return (
            field + DIFFUSION * (up + down + sideways(field))
            + coupling * (1.0 - 3.0 * state * state) * field
        )

    field = advance(field, near[0:1], near[1:2], first)
    adj_out[...] = advance(field, near_next[0:1], near_next[1:2], second)

    for which in range(2):
        h_copy(which).wait_send()
        y_copy(which).wait_send()
    loop(1, PLANE, lambda d: ar_copy(plane_peer(q, z), q, q, d).wait_send())
    loop(1, PLANE, lambda d: ct_copy(plane_peer(q, z), q, q, d).wait_send())
    loop(1, PLANE, lambda d: g_copy(plane_peer(q, z), q, d).wait_send())
    for d in range(1, ZS):
        z_copy(z_peer(z), z, d).wait_send()
        cz_copy(z_peer(z), z, z, d).wait_send()


def shards(snapshots, range_test, test_rows, species, reaction_rates, adjoint_end):
    vmem = pl.BlockSpec(memory_space=pltpu.VMEM)
    smem = pl.BlockSpec(memory_space=pltpu.SMEM)
    hbm = pl.BlockSpec(memory_space=pl.ANY)
    dma = pltpu.SemaphoreType.DMA
    buffer = pltpu.VMEM
    adjoint, factors = pl.pallas_call(
        whole_kernel,
        in_specs=[hbm, hbm, hbm, hbm, smem, hbm],
        out_specs=[vmem] * 2,
        out_shape=[
            jax.ShapeDtypeStruct((8, WIDTH), F32),
            jax.ShapeDtypeStruct((2, 128), F32),
        ],
        scratch_shapes=[
            buffer((STEPS, WIDTH, 512), BF16),
            buffer((STEPS, 256, WIDTH), BF16),
            buffer((512, 128), BF16),
            buffer((8, WIDTH), jnp.int32),
            buffer((8, WIDTH), F32),
            buffer((STEPS, 128, WIDTH), F32),
            buffer((256, 512), F32),
            buffer((256, 256), F32),
            buffer((PLANE, 16, 128), F32),
            buffer((PLANE, 16, 256), F32),
            buffer((PLANE, 16, 128), F32),
            buffer((PLANE, 16, 256), F32),
            buffer((16, 128), F32),
            buffer((ZS, 16, 128), F32),
            buffer((16, 128), F32),
            buffer((PLANE, 16, 128), F32),
            buffer((ZS, 2, 256), F32),
            buffer((ZS, 2, 256), F32),
            buffer((2, 4, WIDTH), F32),
            buffer((2, 4, WIDTH), F32),
            buffer((2, 128, WIDTH), F32),
            dma((STEPS,)), dma((STEPS,)), dma((3,)),
            dma((PLANE,)), dma((PLANE,)), dma((PLANE,)), dma((PLANE,)),
            dma((ZS,)), dma((ZS,)), dma((PLANE,)), dma((PLANE,)),
            dma((ZS,)), dma((ZS,)), dma((2,)), dma((2,)), dma((2,)), dma((2,)),
        ],
        compiler_params=pltpu.CompilerParams(
            collective_id=0, has_side_effects=True, vmem_limit_bytes=56 << 20
        ),
        name="whole",
    )(snapshots, range_test, test_rows, species, reaction_rates, adjoint_end)
    return adjoint, factors.T


def solution(mesh):
    cells = ("space", "tm")
    in_specs = (P(cells, None), P(), P(None, cells), P(cells, None), P(), P(cells, None))
    out_specs = (P(cells, None), P(None, cells))
    return jax.shard_map(
        shards, mesh=mesh, in_specs=in_specs, out_specs=out_specs, check_vma=False
    )
```

time: 410 us -> 58 us (0.14); the launches traced: 405 us -> 57.8 us
  waiting for transfers between devices: 253 us -> 0 us
  Pallas kernels: 0 us -> 54.6 us
  other arithmetic: 48.4 us -> 0 us
  blocking collectives: 39.1 us -> 0 us
  matrix products: 35.5 us -> 0 us
  between operations: 14.4 us -> 0.64 us
  starting transfers between devices: 12.6 us -> 0 us
    psum x1 -> x0, waiting for transfers between devices: 252 us -> none  [together(): running = lax.psum(vector, axis)]
    pallas_call x0 -> x1, Pallas kernels: none -> 54.6 us  [shards(): pl.pallas_call(whole_kernel, in_specs=[hbm, hbm, hbm, hbm, smem, hbm], ou...]
    another operation x10 -> x0, other arithmetic: 45.9 us -> none  [the longest x3 12.6 us: shards(): normal_factor = jnp.linalg.cholesky(normal_matrix)]
    psum x4 -> x0, blocking collectives: 39.1 us -> none  [from_root(): value = lax.psum(value, axis)]
    dot_general x7 -> x0, matrix products: 25.3 us -> none  [the longest x1 6.91 us: shards(): lax.dot_general(range_part, range_part, contract_rows, precision=high)]
    ppermute x4 -> x0, starting transfers between devices: 12.6 us -> none  [the longest x2 7.36 us: with_halo(): lax.ppermute(lax.slice_in_dim(block, 0, width, axis=dim), axis, backward)]
    another operation x4 -> x0, matrix products: 10.1 us -> none  [the longest x1 7.92 us: shards(): jax.scipy.linalg.solve_triangular(lower_factor, range_part.T, lower=True)]
  transfers between devices with their start and end apart: 5 -> 0, of which waited for: 2 -> 0; matrix products, arithmetic and copies ran while one was open for 16% -> 0% of each run, Pallas kernels for 0% -> 0%
where the time goes in v2:
time: 58 us; the launch traced here: 57.8 us
  Pallas kernels  54.6 us (94%)
  local copies, waits for them, and re-layouts  2.6 us (4%)
  between operations  0.64 us (1%)
    pallas_call x1, Pallas kernels, shards(): pl.pallas_call(whole_kernel, in_specs=[hbm, hbm, hbm, hbm, smem, hbm], ou...  54.6 us
    unnamed x2, local copies, waits for them, and re-layouts  2.6 us

profile of v2, /device:TPU:1, one launch (start us, length us, event | category | flops | bytes accessed | tf_op | source)
XLA Modules:
  0.0 57.8 jit_solution(2706514743143487821)
XLA Ops:
  0.6 54.6 %whole.1 = (f32[8,1024]{1,0:T(8,128)}, f32[2,128]{1,0:T(2,128)}) custom-call(bf16[8192,512]{1,0:T(8,128)(2,1)} %x_hbm.1, bf16[512,128]{1,0:T(8,128)(2,1)} %om_hbm.1, bf16[256,8192]{1,0:T(8,128)(2,1)} %psi_hbm.1, s32[8,1024]{1,0:T(8,128)} %spec_hbm.1, f32[4]{0:T(128)} %rates.1, f32[8,1024]{1,0:T(8,128)} %adj_hbm.1), custom_call_target="tpu_custom_call" | custom-call | tf_op jit(solution)/shard_map/whole/pallas_call | solution.py:403
  55.2 1.4 %copy.10 = f32[8,1024]{1,0:T(8,128)} copy(f32[8,1024]{1,0:T(8,128)} %get-tuple-element.8) | data formatting | bytes 65536
  56.6 1.2 %copy.11 = f32[128,2]{0,1:T(2,128)} copy(f32[128,2]{0,1:T(2,128)} %bitcast.1) | data formatting | bytes 2048

commit v3 on v2

v3 whole, which is shorter than its diff:
```python
import functools

import jax
import jax.numpy as jnp
from jax import lax
from jax.experimental import pallas as pl
from jax.experimental.pallas import tpu as pltpu
from jax.sharding import PartitionSpec as P

DIFFUSION = 0.2
STEP_SIZE = 0.05
MESH = pl.DeviceIdType.MESH
HIGH = lax.Precision.HIGHEST
F32 = jnp.float32
BF16 = jnp.bfloat16

YS, ZS, XS, CS = 4, 8, 4, 2
PLANE = YS * XS * CS
STEPS = 8
WIDTH = 1024
AHEAD = 4


def iota(shape, dim):
    return lax.broadcasted_iota(jnp.int32, shape, dim)


def place():
    s = lax.axis_index("space")
    return (
        lax.div(s, ZS * XS), lax.rem(lax.div(s, XS), ZS), lax.rem(s, XS), lax.axis_index("tm")
    )


def lane(a, k):
    return jnp.broadcast_to(a[:, k : k + 1], (8, 128))


def sub(a, k):
    return jnp.broadcast_to(a[k : k + 1, :], (8, 128))


def product(old, k0, pieces):
    terms = [lane(old, k0 + j) * pieces[j] for j in range(8)]
    while len(terms) > 1:
        terms = [terms[i] + terms[i + 1] for i in range(0, len(terms), 2)]
    return terms[0]


def panel_steps(panel, k0, in_place, zero):
    subs, lanes = iota((8, 128), 0), iota((8, 128), 1)
    cols = [lane(panel, k0 + j) + zero for j in range(8)]
    upper = jnp.zeros((8, 128), F32)
    for i in range(8):
        here = subs == i
        pivot = sub(cols[i], i)
        inverse = 1.0 / pivot
        if in_place:
            panel = jnp.where(lanes == k0 + i, jnp.where(here, 1.0, 0.0), panel)
        else:
            upper = jnp.where(here & (lanes >= k0 + i), panel * lax.rsqrt(pivot), upper)
        row = sub(panel, i) * inverse
        panel = jnp.where(here, row, panel - cols[i] * row)
        for j in range(i + 1, 8):
            entry = sub(cols[j], i) * inverse
            cols[j] = jnp.where(here, entry, cols[j] - cols[i] * entry)
        yield
    return panel, upper


def upper_factor(rows, zero, out):
    rows = list(rows)
    for k in range(16):
        k0 = 8 * k
        panel, upper = yield from panel_steps(rows[k], k0, False, zero)
        out.append(upper)
        pieces = [sub(panel, j) for j in range(8)]
        for b in range(k + 1, 16):
            rows[b] = rows[b] - product(rows[b], k0, pieces)
            yield


def solve_rows(rows, right, zero, out):
    rows = list(rows) + [right]
    lanes = iota((8, 128), 1)
    for k in range(16):
        k0 = 8 * k
        inside = (lanes >= k0) & (lanes < k0 + 8)
        panel, _ = yield from panel_steps(rows[k], k0, True, zero)
        panel = jnp.where(inside, -panel, panel)
        pieces = [sub(panel, j) for j in range(8)]
        for b in range(k + 1, 17):
            rows[b] = jnp.where(inside, 0.0, rows[b]) - product(rows[b], k0, pieces)
            yield
    out.append(rows[16])


def in_turn(*works):
    works = list(works)
    while works:
        for work in list(works):
            try:
                next(work)
            except StopIteration:
                works.remove(work)


def sideways(field):
    nothing = jnp.zeros((field.shape[0], 1), F32)
    left = jnp.concatenate([nothing, field[:, :-1]], axis=1)
    right = jnp.concatenate([field[:, 1:], nothing], axis=1)
    return left + right - 4.0 * field


def coupling_of(kinds, rates):
    coupling = jnp.zeros(kinds.shape, F32)
    for kind in range(4):
        coupling = jnp.where(kinds == kind, rates[kind], coupling)
    return coupling


def loop(low, high, body):
    def step(d, carry):
        body(d)
        return carry

    lax.fori_loop(low, high, step, 0)


def whole_kernel(
    x_hbm, om_hbm, psi_hbm, spec_hbm, rates, adj_hbm,
    adj_out, t_out,
    xb, psib, omb, spec, adj, yt, c_acc, k_acc, zeros,
    ar, ct, ct_pair, ct_half, ar_in, ct_in, part, z_in, done, sums, ct_part, ctz_in, edge, halo, halo_y,
    x_sem, psi_sem, small_sem,
    ar_send, ar_recv, ct_send, ct_recv, z_send, z_recv, g_send, g_recv, cz_send, cz_recv,
    h_send, h_recv, y_send, y_recv, p_send, p_recv,
):
    y, z, x, c = place()
    q = (y * XS + x) * CS + c
    me = ((y * ZS + z) * XS + x) * CS + c

    def x_copy(k):
        return pltpu.make_async_copy(
            x_hbm.at[pl.ds(k * WIDTH, WIDTH), :], xb.at[k], x_sem.at[k])

    def psi_copy(k):
        return pltpu.make_async_copy(
            psi_hbm.at[:, pl.ds(k * WIDTH, WIDTH)], psib.at[k], psi_sem.at[k])

    def fetch(k):
        x_copy(k).start()
        psi_copy(k).start()

    om_copy = pltpu.make_async_copy(om_hbm, omb, small_sem.at[0])
    spec_copy = pltpu.make_async_copy(spec_hbm, spec, small_sem.at[1])
    adj_copy = pltpu.make_async_copy(adj_hbm, adj, small_sem.at[2])
    om_copy.start()
    for i in range(AHEAD):
        fetch((i + 7) % STEPS)
    spec_copy.start()
    adj_copy.start()

    y_at = [lax.rem(y + d, YS) for d in range(YS)]
    x_at = [lax.rem(x + d, XS) for d in range(XS)]
    z_at = [lax.rem(z + d, ZS) for d in range(ZS)]
    c_at = [c, 1 - c]
    plane = [
        ((yy * XS + xx) * CS + cc, ((yy * ZS + z) * XS + xx, cc))
        for yy in y_at for xx in x_at for cc in c_at
    ][1:]
    chips = [
        (yy * XS + xx, ((yy * ZS + z) * XS + xx, c)) for yy in y_at for xx in x_at
    ][1:]
    column = [(zz, ((y * ZS + zz) * XS + x, c)) for zz in z_at[1:]]
    after, before = lax.rem(me + 1, 256), lax.rem(me + 255, 256)
    ring = [(lax.div(after, CS), lax.rem(after, CS)), (lax.div(before, CS), lax.rem(before, CS))]

    barrier = pltpu.get_barrier_semaphore()
    for to in [p[1] for p in plane + column] + ring:
        pl.semaphore_signal(barrier, inc=1, device_id=to, device_id_type=MESH)

    def remote(source, target, send, recv, to):
        return pltpu.make_async_remote_copy(
            src_ref=source, dst_ref=target, send_sem=send, recv_sem=recv,
            device_id=to, device_id_type=MESH)

    def all_of(source, target, send, recv, count):
        return remote(source.at[pl.ds(0, count)], target.at[pl.ds(0, count)], send, recv, ring[0])

    def h_copy(which):
        return remote(edge.at[which], halo.at[which], h_send.at[which], h_recv.at[which],
                      ring[which])

    def y_copy(which):
        return remote(yt.at[7 if which == 0 else 0], halo_y.at[which],
                      y_send.at[which], y_recv.at[which], ring[which])

    zeros[...] = jnp.zeros_like(zeros)
    c_acc[...] = jnp.zeros_like(c_acc)
    k_acc[...] = jnp.zeros_like(k_acc)
    om_copy.wait()

    def block(i):
        k = lax.rem(i + 7, STEPS)
        x_copy(k).wait()
        psi_copy(k).wait()
        xs = xb[k]
        ys = jnp.dot(xs, omb[...], preferred_element_type=F32)
        c_acc[...] += jnp.dot(psib[k], xs, preferred_element_type=F32)
        ys_t = ys.T
        yt[k] = ys_t
        hi = ys.astype(BF16)
        lo = (ys - hi.astype(F32)).astype(BF16)
        wide = jnp.concatenate([hi, lo], axis=1)
        k_acc[...] += jnp.dot(ys_t.astype(BF16), wide, preferred_element_type=F32)

    def pair(i):
        ks = [lax.rem(i + 7, STEPS), lax.rem(i + 8, STEPS)]
        turns = []
        for k in ks:
            x_copy(k).wait()
            psi_copy(k).wait()
        for k in ks:
            turns.append(jnp.dot(xb[k], omb[...], preferred_element_type=F32))
        both = jnp.dot(psib[ks[0]], xb[ks[0]], preferred_element_type=F32)
        grams = None
        for n, k in enumerate(ks):
            ys = turns[n]
            ys_t = ys.T
            yt[k] = ys_t
            hi = ys.astype(BF16)
            lo = (ys - hi.astype(F32)).astype(BF16)
            wide = jnp.concatenate([hi, lo], axis=1)
            here = jnp.dot(ys_t.astype(BF16), wide, preferred_element_type=F32)
            if n == 0:
                grams = here
                both = both + jnp.dot(psib[ks[1]], xb[ks[1]], preferred_element_type=F32)
            else:
                grams = grams + here
        c_acc[...] += both
        k_acc[...] += grams

    def early(i):
        fetch(lax.rem(i + 7 + AHEAD, STEPS))
        block(i)

    loop(0, 2, early)
    for i in range(2 + AHEAD, STEPS):
        fetch((i + 7) % STEPS)
    spec_copy.wait()
    adj_copy.wait()
    coupling = coupling_of(spec[...], rates)
    edge[0, 0:1] = adj[7:8, :]
    edge[0, 1:2] = adj[6:7, :]
    edge[0, 2:3] = coupling[7:8, :]
    edge[0, 3:4] = coupling[7:8, :]
    edge[1, 0:1] = adj[0:1, :]
    edge[1, 1:2] = adj[1:2, :]
    edge[1, 2:3] = coupling[0:1, :]
    edge[1, 3:4] = coupling[0:1, :]
    pl.semaphore_wait(barrier, PLANE - 1 + ZS - 1 + 2)
    for which in range(2):
        y_copy(which).start()
        h_copy(which).start()
    loop(1, STEPS // 2, lambda n: pair(2 * n))
    r = 128
    cross = k_acc[:, r:]
    gram = k_acc[:, 0:r] + (cross + cross.T)
    om_f = omb[...]
    c_all = c_acc[...]
    c_1 = c_all.astype(BF16)
    rest = c_all - c_1.astype(F32)
    c_2 = rest.astype(BF16)
    c_3 = (rest - c_2.astype(F32)).astype(BF16)
    raw = (
        jnp.dot(c_3, om_f, preferred_element_type=F32)
        + jnp.dot(c_2, om_f, preferred_element_type=F32)
        + jnp.dot(c_1, om_f, preferred_element_type=F32)
    )
    row = iota((r, r), 0)
    source = ((row >> 1) & 7) * 16 + ((row >> 4) & 3) * 4 + ((row >> 6) & 1) * 2 + (row & 1)
    perm = jnp.where(iota((r, r), 1) == source, 1.0, 0.0).astype(F32)

    def turned(at):
        piece = lax.dot_general(
            perm, c_acc[:, at * r : (at + 1) * r], (((1,), (1,)), ((), ())),
            precision=HIGH, preferred_element_type=F32)
        ct[0, 4 * at : 4 * at + 4] = piece[0:64].reshape(4, 16, 256)
        ct[1, 4 * at : 4 * at + 4] = piece[64:128].reshape(4, 16, 256)

    turned(YS - 1)
    ends = ct[1, 15, 14:16, :]
    carried = jnp.concatenate(
        [ends[i : i + 1, 64 * k : 64 * k + 64] for i in range(2) for k in range(4)], axis=0)
    mixed = jnp.concatenate([carried, gram[64:72, 64:128]], axis=1)
    for p in range(PLANE):
        ar[p, 0] = raw[8 * p : 8 * p + 4]
        ar[p, 1] = raw[8 * p + 4 : 8 * p + 8]
        ar[p, 2] = gram[4 * p : 4 * p + 4] if p not in (16, 17) else (
            mixed[0:4] if p == 16 else mixed[4:8])

    for p, to in plane:
        remote(ar.at[p], ar_in.at[q], ar_send, ar_recv, to).start()
    ar_in[q] = ar[q]
    for at in range(YS - 1):
        turned(at)
    pair_copy = remote(ct.at[1 - c], ct_pair, p_send, p_recv, (lax.axis_index("space"), 1 - c))
    pair_copy.start()
    all_of(ar, ar_in, ar_send, ar_recv, PLANE - 1).wait_recv()
    part[...] = jnp.sum(ar_in[...], axis=0)

    for zz, to in column:
        remote(part, z_in.at[z], z_send, z_recv, to).start()
    pair_copy.wait_recv()
    ct_half[...] = ct[c] + ct_pair[...]
    chip = y * XS + x
    for n, to in chips:
        remote(ct_half.at[n], ct_in.at[chip], ct_send, ct_recv, to).start()
    ct_in[chip] = ct_half[chip]
    z_in[z] = part[...]
    all_of(z_in, z_in, z_send, z_recv, ZS - 1).wait_recv()
    total = jnp.sum(z_in[...], axis=0)
    done[...] = total

    for p, to in plane:
        remote(done, sums.at[q], g_send, g_recv, to).start()
    sums[q] = total

    all_of(ct_half, ct_in, ct_send, ct_recv, YS * XS - 1).wait_recv()
    ct_sum = jnp.sum(ct_in[...], axis=0)
    for zz in range(ZS):
        ct_part[zz] = ct_sum[2 * zz : 2 * zz + 2]
    for zz, to in column:
        remote(ct_part.at[zz], ctz_in.at[z], cz_send, cz_recv, to).start()
    ctz_in[z] = ct_part[z]
    all_of(sums, sums, g_send, g_recv, PLANE - 1).wait_recv()
    all_of(ct_part, ctz_in, cz_send, cz_recv, ZS - 1).wait_recv()
    mine = jnp.sum(ctz_in[...], axis=0)

    raw = jnp.concatenate([sums[p, half] for p in range(PLANE) for half in range(2)], axis=0)
    gram_rows = [
        jnp.concatenate([sums[2 * k, 2], sums[2 * k + 1, 2]], axis=0) for k in range(16)
    ]
    mixed = gram_rows[8]
    last = jnp.concatenate([
        jnp.concatenate([mixed[4 * i + k : 4 * i + k + 1, 0:64] for k in range(4)], axis=1)
        for i in range(2)
    ], axis=0)
    mirror = jnp.concatenate(gram_rows[0:8], axis=0).T[64:72, :]
    gram_rows[8] = jnp.concatenate([mirror, mixed[:, 64:128]], axis=1)
    right = jnp.concatenate([mine, last, jnp.zeros((4, 256), F32)], axis=0)
    right = jnp.dot(right, raw, precision=HIGH)
    normal = lax.dot_general(raw, raw, (((0,), (0,)), ((), ())), precision=HIGH)
    upper, solved = [], []
    zero = zeros[...]
    in_turn(
        solve_rows([normal[8 * k : 8 * k + 8] for k in range(16)], right, zero, solved),
        upper_factor(gram_rows, zero, upper),
    )
    solved = solved[0]
    factor = jnp.concatenate(upper, axis=0)
    times = lax.dot_general(
        solved, factor, (((1,), (1,)), ((), ())), precision=HIGH
    ) * (2097152.0 ** -0.5)
    t_out[...] = times[0:2]
    columns = jnp.concatenate([solved] * 16, axis=0).T

    def state(blocks, j):
        weights = jnp.broadcast_to(columns[:, j : j + 1], (r, r))
        tiles = []
        for b in range(8):
            tiles.append(jnp.concatenate([
                jnp.sum(get(b * r) * weights, axis=0, keepdims=True) for get in blocks
            ], axis=0))
        return jnp.concatenate(tiles, axis=1)

    own = [functools.partial(lambda k, at: yt[k, :, at : at + r], k) for k in range(8)]
    y_copy(0).wait_recv()
    y_copy(1).wait_recv()
    h_copy(0).wait_recv()
    h_copy(1).wait_recv()
    outer = [functools.partial(lambda k, at: halo_y[k, :, at : at + r], k) for k in range(2)]
    first, second, edges = state(own, 3), state(own, 2), state(outer, 3)

    coupling = STEP_SIZE * coupling_of(spec[...], rates)
    field = adj[...]
    near = jnp.concatenate([halo[0, 0:1], halo[1, 0:1]], axis=0)
    far = jnp.concatenate([halo[0, 1:2], halo[1, 1:2]], axis=0)
    rate = jnp.concatenate([halo[0, 2:3], halo[1, 2:3]], axis=0) * STEP_SIZE
    inner = jnp.concatenate([field[0:1], field[7:8]], axis=0)
    side = iota((2, WIDTH), 0)
    absent = ((side == 0) & (me == 0)) | ((side == 1) & (me == 255))
    near = jnp.where(absent, 0.0, near)
    near_next = (
        near + DIFFUSION * (far + inner + sideways(near))
        + rate * (1.0 - 3.0 * edges * edges) * near
    )
    near_next = jnp.where(absent, 0.0, near_next)

    def advance(field, low, high, state):
        up = jnp.concatenate([low, field[0:7]], axis=0)
        down = jnp.concatenate([field[1:8], high], axis=0)
        return (
            field + DIFFUSION * (up + down + sideways(field))
            + coupling * (1.0 - 3.0 * state * state) * field
        )

    field = advance(field, near[0:1], near[1:2], first)
    adj_out[...] = advance(field, near_next[0:1], near_next[1:2], second)

    for which in range(2):
        h_copy(which).wait_send()
        y_copy(which).wait_send()
    all_of(ar, ar_in, ar_send, ar_recv, PLANE - 1).wait_send()
    all_of(ct_half, ct_in, ct_send, ct_recv, YS * XS - 1).wait_send()
    pair_copy.wait_send()
    all_of(sums, sums, g_send, g_recv, PLANE - 1).wait_send()
    all_of(z_in, z_in, z_send, z_recv, ZS - 1).wait_send()
    all_of(ct_part, ctz_in, cz_send, cz_recv, ZS - 1).wait_send()


def pass_kernel(adj, times, adj_out, times_out):
    adj_out[...] = adj[...]
    times_out[...] = times[...]


def shards(snapshots, range_test, test_rows, species, reaction_rates, adjoint_end):
    vmem = pl.BlockSpec(memory_space=pltpu.VMEM)
    smem = pl.BlockSpec(memory_space=pltpu.SMEM)
    hbm = pl.BlockSpec(memory_space=pl.ANY)
    dma = pltpu.SemaphoreType.DMA
    buffer = pltpu.VMEM
    adjoint, factors = pl.pallas_call(
        whole_kernel,
        in_specs=[hbm, hbm, hbm, hbm, smem, hbm],
        out_specs=[vmem] * 2,
        out_shape=[
            jax.ShapeDtypeStruct((8, WIDTH), F32),
            jax.ShapeDtypeStruct((2, 128), F32),
        ],
        scratch_shapes=[
            buffer((STEPS, WIDTH, 512), BF16),
            buffer((STEPS, 256, WIDTH), BF16),
            buffer((512, 128), BF16),
            buffer((8, WIDTH), jnp.int32),
            buffer((8, WIDTH), F32),
            buffer((STEPS, 128, WIDTH), F32),
            buffer((256, 512), F32),
            buffer((128, 256), F32),
            buffer((8, 128), F32),
            buffer((PLANE, 3, 4, 128), F32),
            buffer((2, 16, 16, 256), F32),
            buffer((16, 16, 256), F32),
            buffer((16, 16, 256), F32),
            buffer((PLANE, 3, 4, 128), F32),
            buffer((16, 16, 256), F32),
            buffer((3, 4, 128), F32),
            buffer((ZS, 3, 4, 128), F32),
            buffer((3, 4, 128), F32),
            buffer((PLANE, 3, 4, 128), F32),
            buffer((ZS, 2, 256), F32),
            buffer((ZS, 2, 256), F32),
            buffer((2, 4, WIDTH), F32),
            buffer((2, 4, WIDTH), F32),
            buffer((2, 128, WIDTH), F32),
            dma((STEPS,)), dma((STEPS,)), dma((3,)),
            *([dma] * 10),
            dma((2,)), dma((2,)), dma((2,)), dma((2,)), dma, dma,
        ],
        compiler_params=pltpu.CompilerParams(
            collective_id=0, has_side_effects=True, vmem_limit_bytes=56 << 20
        ),
        name="whole",
    )(snapshots, range_test, test_rows, species, reaction_rates, adjoint_end)
    adjoint, factors = pl.pallas_call(
        pass_kernel,
        in_specs=[vmem] * 2,
        out_specs=[vmem] * 2,
        out_shape=[
            jax.ShapeDtypeStruct((8, WIDTH), F32),
            jax.ShapeDtypeStruct((2, 128), F32),
        ],
        name="pass_on",
    )(adjoint, factors)
    return adjoint, factors.T


def solution(mesh):
    cells = ("space", "tm")
    in_specs = (P(cells, None), P(), P(None, cells), P(cells, None), P(), P(cells, None))
    out_specs = (P(cells, None), P(None, cells))
    return jax.shard_map(
        shards, mesh=mesh, in_specs=in_specs, out_specs=out_specs, check_vma=False
    )
```

time: 58 us -> 44.1 us (0.76)
  Pallas kernels: 54.6 us -> 43.3 us
  local copies, waits for them, and re-layouts: 2.6 us -> 0 us
    pallas_call x1, Pallas kernels: 54.6 us -> 41.9 us  [shards(): pl.pallas_call(whole_kernel, in_specs=[hbm, hbm, hbm, hbm, smem, hbm], ou...]
    unnamed x2 -> x0, local copies, waits for them, and re-layouts: 2.6 us -> none
    pallas_call x0 -> x1, Pallas kernels: none -> 1.38 us  [shards(): pl.pallas_call(pass_kernel, in_specs=[vmem] * 2, out_specs=[vmem] * 2, ou...]
where the time goes in v3:
time: 44.1 us; the launch traced here: 43.9 us
  Pallas kernels  43.3 us (98%)
  between operations  0.64 us (1%)
    pallas_call x1, Pallas kernels, shards(): pl.pallas_call(whole_kernel, in_specs=[hbm, hbm, hbm, hbm, smem, hbm], ou...  41.9 us
    pallas_call x1, Pallas kernels, shards(): pl.pallas_call(pass_kernel, in_specs=[vmem] * 2, out_specs=[vmem] * 2, ou...  1.38 us

profile of v3, /device:TPU:1, one launch (start us, length us, event | category | flops | bytes accessed | tf_op | source)
XLA Modules:
  0.0 43.9 jit_solution(15708725860811733770)
XLA Ops:
  0.6 41.9 %whole.1 = (f32[8,1024]{1,0:T(8,128)}, f32[2,128]{1,0:T(2,128)}) custom-call(bf16[8192,512]{1,0:T(8,128)(2,1)} %x_hbm.1, bf16[512,128]{1,0:T(8,128)(2,1)} %om_hbm.1, bf16[256,8192]{1,0:T(8,128)(2,1)} %psi_hbm.1, s32[8,1024]{1,0:T(8,128)} %spec_hbm.1, f32[4]{0:T(128)} %rates.1, f32[8,1024]{1,0:T(8,128)} %adj_hbm.1), custom_call_target="tpu_custom_call" | custom-call | tf_op jit(solution)/shard_map/whole/pallas_call | solution.py:434
  42.5 1.4 %pass_on.1 = (f32[8,1024]{1,0:T(8,128)}, f32[2,128]{1,0:T(2,128)}) custom-call(f32[8,1024]{1,0:T(8,128)} %get-tuple-element.6.adj, f32[2,128]{1,0:T(2,128)} %get-tuple-element.7.times), custom_call_target="tpu_custom_call" | custom-call | tf_op jit(solution)/shard_map/pass_on/pallas_call | solution.py:476

commit v4 on v3

--- a/solution.py
+++ b/solution.py
@@ -68,31 +68,61 @@
     return panel, upper
 
 
+def split(value):
+    one = value.astype(BF16).astype(F32)
+    rest = value - one
+    two = rest.astype(BF16).astype(F32)
+    return one, two, rest - two
+
+
+def outer(left, right):
+    a, b, c = split(left)
+    d, e, f = split(right)
+    wide = jnp.concatenate([a, a, b, a, b, c], axis=0).astype(BF16)
+    tall = jnp.concatenate([d, e, d, f, e, d], axis=0).astype(BF16)
+    return lax.dot_general(
+        wide, tall, (((0,), (0,)), ((), ())), preferred_element_type=F32)
+
+
 def upper_factor(rows, zero, out):
     rows = list(rows)
     for k in range(16):
         k0 = 8 * k
-        panel, upper = yield from panel_steps(rows[k], k0, False, zero)
+        old = rows[k]
+        panel, upper = yield from panel_steps(old, k0, False, zero)
         out.append(upper)
-        pieces = [sub(panel, j) for j in range(8)]
-        for b in range(k + 1, 16):
-            rows[b] = rows[b] - product(rows[b], k0, pieces)
+        if k < 15:
+            pieces = [sub(panel, j) for j in range(8)]
+            rows[k + 1] = rows[k + 1] - product(rows[k + 1], k0, pieces)
             yield
+        if k < 14:
+            update = outer(old, panel)
+            for b in range(k + 2, 16):
+                rows[b] = rows[b] - update[8 * b : 8 * b + 8]
+            yield
 
 
 def solve_rows(rows, right, zero, out):
-    rows = list(rows) + [right]
+    rows = list(rows)
     lanes = iota((8, 128), 1)
     for k in range(16):
         k0 = 8 * k
         inside = (lanes >= k0) & (lanes < k0 + 8)
-        panel, _ = yield from panel_steps(rows[k], k0, True, zero)
+        old = rows[k]
+        panel, _ = yield from panel_steps(old, k0, True, zero)
         panel = jnp.where(inside, -panel, panel)
         pieces = [sub(panel, j) for j in range(8)]
-        for b in range(k + 1, 17):
-            rows[b] = jnp.where(inside, 0.0, rows[b]) - product(rows[b], k0, pieces)
+        if k < 15:
+            rows[k + 1] = jnp.where(inside, 0.0, rows[k + 1]) - product(rows[k + 1], k0, pieces)
             yield
-    out.append(rows[16])
+        right = jnp.where(inside, 0.0, right) - product(right, k0, pieces)
+        yield
+        if k < 14:
+            update = outer(old, panel)
+            for b in range(k + 2, 16):
+                rows[b] = jnp.where(inside, 0.0, rows[b]) - update[8 * b : 8 * b + 8]
+            yield
+    out.append(right)
 
 
 def in_turn(*works):
@@ -165,14 +195,16 @@
     x_at = [lax.rem(x + d, XS) for d in range(XS)]
     z_at = [lax.rem(z + d, ZS) for d in range(ZS)]
     c_at = [c, 1 - c]
+    near = [(2, 2), (1, 2), (2, 1), (2, 3), (3, 2), (0, 2), (1, 1), (1, 3), (2, 0), (3, 1), (3, 3), (0, 1), (0, 3), (1, 0), (3, 0)]
     plane = [
-        ((yy * XS + xx) * CS + cc, ((yy * ZS + z) * XS + xx, cc))
-        for yy in y_at for xx in x_at for cc in c_at
-    ][1:]
+        ((y_at[dy] * XS + x_at[dx]) * CS + cc,
+         ((y_at[dy] * ZS + z) * XS + x_at[dx], cc))
+        for dy, dx in near for cc in c_at
+    ] + [((y * XS + x) * CS + 1 - c, (lax.axis_index("space"), 1 - c))]
     chips = [
-        (yy * XS + xx, ((yy * ZS + z) * XS + xx, c)) for yy in y_at for xx in x_at
-    ][1:]
-    column = [(zz, ((y * ZS + zz) * XS + x, c)) for zz in z_at[1:]]
+        (y_at[dy] * XS + x_at[dx], ((y_at[dy] * ZS + z) * XS + x_at[dx], c)) for dy, dx in near
+    ]
+    column = [(zz, ((y * ZS + zz) * XS + x, c)) for zz in [z_at[d] for d in [4, 3, 5, 2, 6, 1, 7]]]
     after, before = lax.rem(me + 1, 256), lax.rem(me + 255, 256)
     ring = [(lax.div(after, CS), lax.rem(after, CS)), (lax.div(before, CS), lax.rem(before, CS))]
 

time: 44.1 us -> 42.2 us (0.957)
  Pallas kernels: 43.3 us -> 41.4 us
    pallas_call x1, Pallas kernels: 41.9 us -> 40 us  [shards(): pl.pallas_call(whole_kernel, in_specs=[hbm, hbm, hbm, hbm, smem, hbm], ou...]
where the time goes in v4:
time: 42.2 us; the launch traced here: 42 us
  Pallas kernels  41.4 us (98%)
  between operations  0.64 us (2%)
    pallas_call x1, Pallas kernels, shards(): pl.pallas_call(whole_kernel, in_specs=[hbm, hbm, hbm, hbm, smem, hbm], ou...  40 us
    pallas_call x1, Pallas kernels, shards(): pl.pallas_call(pass_kernel, in_specs=[vmem] * 2, out_specs=[vmem] * 2, ou...  1.38 us

profile of v4, /device:TPU:1, one launch (start us, length us, event | category | flops | bytes accessed | tf_op | source)
XLA Modules:
  0.0 42.0 jit_solution(2197209260549484895)
XLA Ops:
  0.6 40.0 %whole.1 = (f32[8,1024]{1,0:T(8,128)}, f32[2,128]{1,0:T(2,128)}) custom-call(bf16[8192,512]{1,0:T(8,128)(2,1)} %x_hbm.1, bf16[512,128]{1,0:T(8,128)(2,1)} %om_hbm.1, bf16[256,8192]{1,0:T(8,128)(2,1)} %psi_hbm.1, s32[8,1024]{1,0:T(8,128)} %spec_hbm.1, f32[4]{0:T(128)} %rates.1, f32[8,1024]{1,0:T(8,128)} %adj_hbm.1), custom_call_target="tpu_custom_call" | custom-call | tf_op jit(solution)/shard_map/whole/pallas_call | solution.py:466
  40.7 1.4 %pass_on.1 = (f32[8,1024]{1,0:T(8,128)}, f32[2,128]{1,0:T(2,128)}) custom-call(f32[8,1024]{1,0:T(8,128)} %get-tuple-element.6.adj, f32[2,128]{1,0:T(2,128)} %get-tuple-element.7.times), custom_call_target="tpu_custom_call" | custom-call | tf_op jit(solution)/shard_map/pass_on/pallas_call | solution.py:508

commit v5 on v4

--- a/solution.py
+++ b/solution.py
@@ -468,8 +468,8 @@
         in_specs=[hbm, hbm, hbm, hbm, smem, hbm],
         out_specs=[vmem] * 2,
         out_shape=[
-            jax.ShapeDtypeStruct((8, WIDTH), F32),
-            jax.ShapeDtypeStruct((2, 128), F32),
+            pltpu.VMEM((8, WIDTH), F32),
+            pltpu.VMEM((2, 128), F32),
         ],
         scratch_shapes=[
             buffer((STEPS, WIDTH, 512), BF16),
@@ -514,7 +514,10 @@
             jax.ShapeDtypeStruct((2, 128), F32),
         ],
         name="pass_on",
-    )(adjoint, factors)
+    )(
+        pltpu.with_memory_space_constraint(adjoint, pltpu.VMEM),
+        pltpu.with_memory_space_constraint(factors, pltpu.VMEM),
+    )
     return adjoint, factors.T
 
 

time: 42.2 us -> 40.8 us (0.967)
  Pallas kernels: 41.4 us -> 40 us
    pallas_call x1, Pallas kernels: 1.38 us -> 0.62 us  [shards(): pl.pallas_call(pass_kernel, in_specs=[vmem] * 2, out_specs=[vmem] * 2, ou...]
    pallas_call x1, Pallas kernels: 40 us -> 39.4 us  [shards(): pl.pallas_call(whole_kernel, in_specs=[hbm, hbm, hbm, hbm, smem, hbm], ou...]
where the time goes in v5:
time: 40.8 us; the launch traced here: 40.7 us
  Pallas kernels  40 us (98%)
  between operations  0.64 us (2%)
    pallas_call x1, Pallas kernels, shards(): pl.pallas_call(whole_kernel, in_specs=[hbm, hbm, hbm, hbm, smem, hbm], ou...  39.4 us

profile of v5, /device:TPU:1, one launch (start us, length us, event | category | flops | bytes accessed | tf_op | source)
XLA Modules:
  0.0 40.7 jit_solution(2027519803866807724)
XLA Ops:
  0.6 39.4 %whole.1 = (f32[8,1024]{1,0:T(8,128)S(1)}, f32[2,128]{1,0:T(2,128)S(1)}) custom-call(bf16[8192,512]{1,0:T(8,128)(2,1)} %x_hbm.1, bf16[512,128]{1,0:T(8,128)(2,1)} %om_hbm.1, bf16[256,8192]{1,0:T(8,128)(2,1)} %psi_hbm.1, s32[8,1024]{1,0:T(8,128)} %spec_hbm.1, f32[4]{0:T(128)} %rates.1, f32[8,1024]{1,0:T(8,128)} %adj_hbm.1), custom_call_target="tpu_custom_call" | custom-call | tf_op jit(solution)/shard_map/whole/pallas_call | solution.py:466
  40.0 0.6 %pass_on.1 = (f32[8,1024]{1,0:T(8,128)}, f32[2,128]{1,0:T(2,128)}) custom-call(f32[8,1024]{1,0:T(8,128)S(1)} %get-tuple-element.6.adj, f32[2,128]{1,0:T(2,128)S(1)} %get-tuple-element.7.times), custom_call_target="tpu_custom_call" | custom-call | tf_op jit(solution)/shard_map/pass_on/pallas_call | solution.py:508

commit v6 on v5

--- a/solution.py
+++ b/solution.py
@@ -224,9 +224,10 @@
         return remote(edge.at[which], halo.at[which], h_send.at[which], h_recv.at[which],
                       ring[which])
 
-    def y_copy(which):
-        return remote(yt.at[7 if which == 0 else 0], halo_y.at[which],
-                      y_send.at[which], y_recv.at[which], ring[which])
+    def y_copy(which, half):
+        rows = pl.ds(64 * half, 64)
+        return remote(yt.at[7 if which == 0 else 0, rows], halo_y.at[which, rows],
+                      y_send.at[2 * half + which], y_recv.at[2 * half + which], ring[which])
 
     zeros[...] = jnp.zeros_like(zeros)
     c_acc[...] = jnp.zeros_like(c_acc)
@@ -293,7 +294,7 @@
     edge[1, 3:4] = coupling[0:1, :]
     pl.semaphore_wait(barrier, PLANE - 1 + ZS - 1 + 2)
     for which in range(2):
-        y_copy(which).start()
+        y_copy(which, 0).start()
         h_copy(which).start()
     loop(1, STEPS // 2, lambda n: pair(2 * n))
     r = 128
@@ -321,8 +322,7 @@
         ct[0, 4 * at : 4 * at + 4] = piece[0:64].reshape(4, 16, 256)
         ct[1, 4 * at : 4 * at + 4] = piece[64:128].reshape(4, 16, 256)
 
-    turned(YS - 1)
-    ends = ct[1, 15, 14:16, :]
+    ends = c_acc[:, 3 * r : 4 * r].T[r - 2 : r, :]
     carried = jnp.concatenate(
         [ends[i : i + 1, 64 * k : 64 * k + 64] for i in range(2) for k in range(4)], axis=0)
     mixed = jnp.concatenate([carried, gram[64:72, 64:128]], axis=1)
@@ -335,7 +335,7 @@
     for p, to in plane:
         remote(ar.at[p], ar_in.at[q], ar_send, ar_recv, to).start()
     ar_in[q] = ar[q]
-    for at in range(YS - 1):
+    for at in range(YS):
         turned(at)
     pair_copy = remote(ct.at[1 - c], ct_pair, p_send, p_recv, (lax.axis_index("space"), 1 - c))
     pair_copy.start()
@@ -366,6 +366,8 @@
     for zz, to in column:
         remote(ct_part.at[zz], ctz_in.at[z], cz_send, cz_recv, to).start()
     ctz_in[z] = ct_part[z]
+    for which in range(2):
+        y_copy(which, 1).start()
     all_of(sums, sums, g_send, g_recv, PLANE - 1).wait_recv()
     all_of(ct_part, ctz_in, cz_send, cz_recv, ZS - 1).wait_recv()
     mine = jnp.sum(ctz_in[...], axis=0)
@@ -387,8 +389,8 @@
     upper, solved = [], []
     zero = zeros[...]
     in_turn(
+        upper_factor(gram_rows, zero, upper),
         solve_rows([normal[8 * k : 8 * k + 8] for k in range(16)], right, zero, solved),
-        upper_factor(gram_rows, zero, upper),
     )
     solved = solved[0]
     factor = jnp.concatenate(upper, axis=0)
@@ -408,8 +410,9 @@
         return jnp.concatenate(tiles, axis=1)
 
     own = [functools.partial(lambda k, at: yt[k, :, at : at + r], k) for k in range(8)]
-    y_copy(0).wait_recv()
-    y_copy(1).wait_recv()
+    for half in range(2):
+        y_copy(0, half).wait_recv()
+        y_copy(1, half).wait_recv()
     h_copy(0).wait_recv()
     h_copy(1).wait_recv()
     outer = [functools.partial(lambda k, at: halo_y[k, :, at : at + r], k) for k in range(2)]
@@ -443,7 +446,8 @@
 
     for which in range(2):
         h_copy(which).wait_send()
-        y_copy(which).wait_send()
+        y_copy(which, 0).wait_send()
+        y_copy(which, 1).wait_send()
     all_of(ar, ar_in, ar_send, ar_recv, PLANE - 1).wait_send()
     all_of(ct_half, ct_in, ct_send, ct_recv, YS * XS - 1).wait_send()
     pair_copy.wait_send()
@@ -498,7 +502,7 @@
             buffer((2, 128, WIDTH), F32),
             dma((STEPS,)), dma((STEPS,)), dma((3,)),
             *([dma] * 10),
-            dma((2,)), dma((2,)), dma((2,)), dma((2,)), dma, dma,
+            dma((2,)), dma((2,)), dma((4,)), dma((4,)), dma, dma,
         ],
         compiler_params=pltpu.CompilerParams(
             collective_id=0, has_side_effects=True, vmem_limit_bytes=56 << 20

time: 40.8 us -> 39.5 us (0.968); the launches traced: 40.7 us -> 38.8 us
  Pallas kernels: 40 us -> 38.2 us
    pallas_call x1, Pallas kernels: 39.4 us -> 37.6 us  [shards(): pl.pallas_call(whole_kernel, in_specs=[hbm, hbm, hbm, hbm, smem, hbm], ou...]
where the time goes in v6:
time: 39.5 us; the launch traced here: 38.8 us
  Pallas kernels  38.2 us (97%)
  between operations  0.64 us (2%)
    pallas_call x1, Pallas kernels, shards(): pl.pallas_call(whole_kernel, in_specs=[hbm, hbm, hbm, hbm, smem, hbm], ou...  37.6 us

profile of v6, /device:TPU:1, one launch (start us, length us, event | category | flops | bytes accessed | tf_op | source)
XLA Modules:
  0.0 38.8 jit_solution(2771551578529824550)
XLA Ops:
  0.6 37.6 %whole.1 = (f32[8,1024]{1,0:T(8,128)S(1)}, f32[2,128]{1,0:T(2,128)S(1)}) custom-call(bf16[8192,512]{1,0:T(8,128)(2,1)} %x_hbm.1, bf16[512,128]{1,0:T(8,128)(2,1)} %om_hbm.1, bf16[256,8192]{1,0:T(8,128)(2,1)} %psi_hbm.1, s32[8,1024]{1,0:T(8,128)} %spec_hbm.1, f32[4]{0:T(128)} %rates.1, f32[8,1024]{1,0:T(8,128)} %adj_hbm.1), custom_call_target="tpu_custom_call" | custom-call | tf_op jit(solution)/shard_map/whole/pallas_call | solution.py:470
  38.2 0.6 %pass_on.1 = (f32[8,1024]{1,0:T(8,128)}, f32[2,128]{1,0:T(2,128)}) custom-call(f32[8,1024]{1,0:T(8,128)S(1)} %get-tuple-element.6.adj, f32[2,128]{1,0:T(2,128)S(1)} %get-tuple-element.7.times), custom_call_target="tpu_custom_call" | custom-call | tf_op jit(solution)/shard_map/pass_on/pallas_call | solution.py:512
